TPU v7x, 512 devices: a whole 4x4x16 slice. The times are simulated.
512 devices in a mesh: parts: 512 (over z, y, x, core).
Axes of the slice: x: 4, y: 4, z: 16, core: 2. Of those that a mesh axis runs over, the one named last changes fastest.
Arguments:
- positions: float32 [3, 262144], P(None, 'parts'), may hold values from -6 to 6
- velocity: float32 [3, 262144], P(None, 'parts'), may hold values from -6 to 6
- inv_mass: float32 [262144], P('parts'), may hold values from 0.5 to 4
- swap_lists: int32 [3, 131072], P(None, 'parts'), may hold values from 0 to 511, as said below
- rim_list: int32 [65536], P('parts'), may hold values from 0 to 511, as said below
- contact_pair: int32 [2, 524288], P(None, 'parts'), may hold values from 0 to 767, as said below
- delassus: float32 [4096, 128, 128], P('parts'), as said below
Outputs:
- new_velocity: float32 [3, 262144], P(None, 'parts')
- impulse: float32 [524288], P('parts')
Inputs may be any that keep to these rules, and one draw needn't show every extreme that they name: `swap_lists`: the 256 slots of one part at one level are distinct. `rim_list`: the 128 slots of one part are distinct. `contact_pair`: the first index of a contact is a local grain; the two indices differ. `delassus`: tile diagonals lie between 4 and 8.
All inputs are finite; a program needn't handle non-finite values.
Results may differ from a plain program's by a relative error of at most 0.0003.
Values sent between devices are 32-bit elements; how exact they have to be, the bound alone decides.
A program may use at most 64 MiB of HBM per device.

v0:
```python
import jax
import jax.numpy as jnp
from jax import lax
from jax.sharding import PartitionSpec as P

TILE = 128
LEVELS = 3
ITERS = 2


def partner(value, axis, apart):
    mask = 2**apart
    pairs = [(source, source ^ mask) for source in range(lax.axis_size(axis))]
    return lax.ppermute(value, axis, pairs)


def with_halo(x, sides, width):
    for axis, dim in sides:
        size, length = (lax.axis_size(axis), x.shape[dim])
        up = [(i, (i + 1) % size) for i in range(size - 1)]
        down = [(j, i) for i, j in up]
        last = lax.slice_in_dim(x, length - width, length, axis=dim)
        first = lax.slice_in_dim(x, 0, width, axis=dim)
        before = lax.ppermute(last, axis, up)
        after = lax.ppermute(first, axis, down)
        x = jnp.concatenate([before, x, after], axis=dim)
    return x


def selector(slots, extent):
    return (slots[:, None] == jnp.arange(extent, dtype=jnp.int32)[None, :]).astype(jnp.float32)


def pick(field, table):
    return lax.dot_general(
        field,
        table,
        (((1,), (1,)), ((), ())),
        precision=lax.Precision.HIGHEST,
        preferred_element_type=jnp.float32,
    )


def spread(values, table):
    return jnp.dot(
        values, table, precision=lax.Precision.HIGHEST, preferred_element_type=jnp.float32
    )


def attach(field, halo_rows, width):
    return jnp.concatenate([field, halo_rows[:, :width], halo_rows[:, 2 * width :]], axis=1)


def body(positions, velocity, inv_mass, swap_lists, rim_list, contact_pair, delassus):
    grains = positions.shape[1]
    width = rim_list.shape[0]
    contacts = contact_pair.shape[1]
    tiles = delassus.shape[0]
    extent = grains + 2 * width
    bits = lax.axis_size("parts").bit_length() - 1
    state = jnp.concatenate([positions, velocity, inv_mass[None]], axis=0)
    for level in range(LEVELS):
        table = selector(swap_lists[level], grains)
        arrived = partner(pick(state, table), "parts", bits - 1 - level)
        keep_mask = 1.0 - jnp.sum(table, axis=0)
        state = state * keep_mask[None] + spread(arrived, table)
    vel = state[3:6]
    mass = state[6]
    rim_table = selector(rim_list, grains)
    first_table = selector(contact_pair[0], extent)
    second_table = selector(contact_pair[1], extent)
    neighbour = with_halo(pick(state[0:6], rim_table), (("parts", 1),), width)
    extended = attach(state[0:6], neighbour, width)
    ends = pick(extended, first_table) - pick(extended, second_table)
    normal = ends[0:3]
    relative = ends[3:6]
    diag = jnp.diagonal(delassus, axis1=1, axis2=2).reshape(contacts)
    lam = jnp.zeros((contacts,), jnp.float32)
    current = vel
    for step in range(ITERS):
        if step > 0:
            fresh = with_halo(pick(current, rim_table), (("parts", 1),), width)
            ext_vel = attach(current, fresh, width)
            relative = pick(ext_vel, first_table) - pick(ext_vel, second_table)
        speed = jnp.sum(normal * relative, axis=0)
        coupled = jnp.einsum(
            "tij,tj->ti", delassus, lam.reshape(tiles, TILE), precision=lax.Precision.HIGHEST
        ).reshape(contacts)
        lam = jnp.maximum(0.0, lam - (coupled + speed) / diag)
        force = normal * lam[None]
        partial_value = spread(force, first_table) - spread(force, second_table)
        shared = with_halo(partial_value[:, grains:], (("parts", 1),), width)
        incoming = shared[:, :width] + shared[:, 3 * width :]
        local = partial_value[:, :grains] + spread(incoming, rim_table)
        current = vel + mass[None] * local
    return (current, lam)


def solution(mesh):
    in_specs = (
        P(None, "parts"),
        P(None, "parts"),
        P("parts"),
        P(None, "parts"),
        P("parts"),
        P(None, "parts"),
        P("parts", None, None),
    )
    out_specs = (P(None, "parts"), P("parts"))
    return jax.shard_map(body, mesh=mesh, in_specs=in_specs, out_specs=out_specs, check_vma=False)
```

profile of v0, /device:TPU:127, one launch (start us, length us, event | category | flops | bytes accessed | tf_op | source)
XLA Modules:
  0.0 110.0 jit_solution(1214475980789388332)
XLA Ops:
  2.6 12.8 %collective-permute-start = (f32[7,256]{1,0:T(8,128)S(1)}, f32[7,256]{1,0:T(8,128)S(1)}, u32[]{:S(2)}, u32[]{:S(2)}) collective-permute-start(f32[7,256]{1,0:T(8,128)S(1)} %fusion.30), channel_id=1, source_target_pairs={{0,256},{1,257},{2,258},{3,259},{4,260},{5,261},{6,262},{7,263},{8... | collective-permute-start | bytes 21512 | tf_op jit(solution)/shard_map/ppermute | solution.py:14
  18.0 8.0 %collective-permute-start.1 = (f32[7,256]{1,0:T(8,128)S(1)}, f32[7,256]{1,0:T(8,128)S(1)}, u32[]{:S(2)}, u32[]{:S(2)}) collective-permute-start(f32[7,256]{1,0:T(8,128)S(1)} %fusion.29), channel_id=1, source_target_pairs={{0,128},{1,129},{2,130},{3,131},{4,132},{5,133},{6,134},{7,135},{8... | collective-permute-start | bytes 21512 | tf_op jit(solution)/shard_map/ppermute | solution.py:14
  27.7 2.4 %collective-permute-start.2 = (f32[7,256]{1,0:T(8,128)S(1)}, f32[7,256]{1,0:T(8,128)S(1)}, u32[]{:S(2)}, u32[]{:S(2)}) collective-permute-start(f32[7,256]{1,0:T(8,128)S(1)} %fusion.27), channel_id=1, source_target_pairs={{0,64},{1,65},{2,66},{3,67},{4,68},{5,69},{6,70},{7,71},{8,72},{9,... | collective-permute-start | bytes 21512 | tf_op jit(solution)/shard_map/ppermute | solution.py:14
  30.1 1.2 %multiply_reduce_fusion = f32[8,128]{1,0:T(8,128)S(1)} fusion(f32[8,128,128]{2,1,0:T(8,128)} %param.13), kind=kLoop, calls=%fused_computation.32 | loop fusion | flops 261120 | bytes 528384 | tf_op jit(solution)/shard_map/tij,tj->ti/dot_general | solution.py:86
  31.4 1.6 %collective-permute-done.2 = f32[7,256]{1,0:T(8,128)S(1)} collective-permute-done((f32[7,256]{1,0:T(8,128)S(1)}, f32[7,256]{1,0:T(8,128)S(1)}, u32[]{:S(2)}, u32[]{:S(2)}) %collective-permute-start.2) | collective-permute-done | bytes 7200 | tf_op jit(solution)/shard_map/ppermute | solution.py:14
  34.2 5.8 %collective-permute-start.4 = (f32[6,128]{1,0:T(8,128)S(1)}, f32[6,128]{1,0:T(8,128)S(1)}, u32[]{:S(2)}, u32[]{:S(2)}) collective-permute-start(f32[6,128]{1,0:T(8,128)S(1)} %fusion.32), channel_id=1, source_target_pairs={{1,0},{2,1},{3,2},{4,3},{5,4},{6,5},{7,6},{8,7},{9,8},{10,9},{11,1... | collective-permute-start | bytes 9224 | tf_op jit(solution)/shard_map/ppermute | solution.py:25
  40.1 5.2 %collective-permute-start.3 = (f32[6,128]{1,0:T(8,128)S(1)}, f32[6,128]{1,0:T(8,128)S(1)}, u32[]{:S(2)}, u32[]{:S(2)}) collective-permute-start(f32[6,128]{1,0:T(8,128)S(1)} %fusion.32), channel_id=1, source_target_pairs={{0,1},{1,2},{2,3},{3,4},{4,5},{5,6},{6,7},{7,8},{8,9},{9,10},{10,1... | collective-permute-start | bytes 9224 | tf_op jit(solution)/shard_map/ppermute | solution.py:24
  45.3 5.9 %copy.15 = f32[8,128,128]{0,2,1:T(8,128)} copy(f32[8,128,128]{2,1,0:T(8,128)} %param.13) | data formatting | bytes 1048576 | tf_op args[6]
  51.2 1.8 %gather_fusion = f32[128,8]{1,0:T(8,128)S(1)} fusion(f32[8,128,128]{0,2,1:T(8,128)} %copy.15, s32[128]{0:T(128)S(1)} %or_bitcast_fusion), kind=kCustom, calls=%fused_computation | custom fusion | bytes 9216 | tf_op jit(solution)/shard_map/jit(diagonal)/gather | solution.py:77
  53.1 1.5 %fusion.3 = f32[6,1024]{1,0:T(8,128)S(1)} fusion(s32[1024]{0:T(1024)S(1)} %bitcast.59, f32[6,128]{1,0:T(8,128)S(1)} %collective-permute-done.4, f32[6,128]{1,0:T(8,128)S(1)} %collective-permute-done.3, f32[6,512]{1,0:T(8,128)S(1)} %bitcast.65), kind=kOutput, calls=%fused_computation.5 | convolution fusion | flops 57418752 | bytes 47104 | tf_op jit(solution)/shard_map/dot_general | solution.py:35
  54.7 1.6 %fusion.16 = f32[6,1024]{1,0:T(8,128)S(1)} fusion(f32[6,1024]{1,0:T(8,128)S(1)} %fusion.3, s32[1024]{0:T(1024)S(1)} %bitcast.55, f32[6,128]{1,0:T(8,128)S(1)} %collective-permute-done.4, f32[6,128]{1,0:T(8,128)S(1)} %collective-permute-done.3, f32[6,512]{1,0:T(8,128)S(1)} %bitcast.66), kind=kOutput, calls=%fused_computation.19 | convolution fusion | flops 57424896 | bytes 71680 | tf_op jit(solution)/shard_map/dot_general | solution.py:35
  57.5 1.1 %fusion.19 = f32[3,768]{1,0:T(4,128)S(1)} fusion(f32[3,768]{1,0:T(4,128)S(1)} %fusion.2, s32[1024]{0:T(1024)S(1)} %bitcast.56, f32[1024]{0:T(1024)S(1)} %fusion.57, f32[6,1024]{1,0:T(8,128)S(1)} %fusion.16), kind=kOutput, calls=%fused_computation.23 | convolution fusion | flops 29103360 | bytes 46080 | tf_op jit(solution)/shard_map/dot_general | solution.py:45
  58.7 2.5 %collective-permute-start.5 = (f32[3,128]{1,0:T(4,128)S(1)}, f32[3,128]{1,0:T(4,128)S(1)}, u32[]{:S(2)}, u32[]{:S(2)}) collective-permute-start(f32[3,128]{1,0:T(4,128)S(1)} %get-tuple-element.5), channel_id=1, source_target_pairs={{0,1},{1,2},{2,3},{3,4},{4,5},{5,6},{6,7},{7,8},{8,9},{9,10},{10,1... | collective-permute-start | bytes 4616 | tf_op jit(solution)/shard_map/ppermute | solution.py:24
  61.2 1.9 %collective-permute-start.6 = (f32[3,128]{1,0:T(4,128)S(1)}, f32[3,128]{1,0:T(4,128)S(1)}, u32[]{:S(2)}, u32[]{:S(2)}) collective-permute-start(f32[3,128]{1,0:T(4,128)S(1)} %get-tuple-element.4), channel_id=1, source_target_pairs={{1,0},{2,1},{3,2},{4,3},{5,4},{6,5},{7,6},{8,7},{9,8},{10,9},{11,1... | collective-permute-start | bytes 4616 | tf_op jit(solution)/shard_map/ppermute | solution.py:25
  63.2 8.3 %collective-permute-done.6 = f32[3,128]{1,0:T(4,128)S(1)} collective-permute-done((f32[3,128]{1,0:T(4,128)S(1)}, f32[3,128]{1,0:T(4,128)S(1)}, u32[]{:S(2)}, u32[]{:S(2)}) %collective-permute-start.6) | collective-permute-done | bytes 1568 | tf_op jit(solution)/shard_map/ppermute | solution.py:25
  72.0 2.0 %collective-permute-start.8 = (f32[3,128]{1,0:T(4,128)S(1)}, f32[3,128]{1,0:T(4,128)S(1)}, u32[]{:S(2)}, u32[]{:S(2)}) collective-permute-start(f32[3,128]{1,0:T(4,128)S(1)} %fusion.31), channel_id=1, source_target_pairs={{1,0},{2,1},{3,2},{4,3},{5,4},{6,5},{7,6},{8,7},{9,8},{10,9},{11,1... | collective-permute-start | bytes 4616 | tf_op jit(solution)/shard_map/ppermute | solution.py:25
  74.0 9.3 %collective-permute-start.7 = (f32[3,128]{1,0:T(4,128)S(1)}, f32[3,128]{1,0:T(4,128)S(1)}, u32[]{:S(2)}, u32[]{:S(2)}) collective-permute-start(f32[3,128]{1,0:T(4,128)S(1)} %fusion.31), channel_id=1, source_target_pairs={{0,1},{1,2},{2,3},{3,4},{4,5},{5,6},{6,7},{7,8},{8,9},{9,10},{10,1... | collective-permute-start | bytes 4616 | tf_op jit(solution)/shard_map/ppermute | solution.py:24
  84.2 1.6 %fusion.1 = f32[3,1024]{1,0:T(4,128)S(1)} fusion(s32[1024]{0:T(1024)S(1)} %bitcast.61, f32[3,128]{1,0:T(4,128)S(1)} %collective-permute-done.8, f32[3,128]{1,0:T(4,128)S(1)} %collective-permute-done.7, f32[3,512]{1,0:T(4,128)S(1)} %fusion.25), kind=kOutput, calls=%fused_computation.3 | convolution fusion | flops 29102592 | bytes 25600 | tf_op jit(solution)/shard_map/dot_general | solution.py:35
  85.8 1.6 %fusion.21 = f32[1024]{0:T(1024)S(1)} fusion(f32[3,1024]{1,0:T(4,128)S(1)} %fusion.1, s32[1024]{0:T(1024)S(1)} %bitcast.57, f32[6,1024]{1,0:T(8,128)S(1)} %fusion.16, f32[3,128]{1,0:T(4,128)S(1)} %collective-permute-done.8, f32[3,128]{1,0:T(4,128)S(1)} %collective-permute-done.7, f32[3,512]{1,0:T(4,128)S(1)} %fusion.25), kind=kOutput, calls=%fused_computation.25 | convolution fusion | flops 29110784 | bytes 41984 | tf_op jit(solution)/shard_map/dot_general | solution.py:35
  87.4 1.1 %fusion = f32[3,768]{1,0:T(4,128)S(1)} fusion(s32[1024]{0:T(1024)S(1)} %bitcast.62, f32[1024]{0:T(1024)S(1)} %fusion.59, f32[6,1024]{1,0:T(8,128)S(1)} %fusion.16), kind=kOutput, calls=%fused_computation.2 | convolution fusion | flops 29101056 | bytes 33792 | tf_op jit(solution)/shard_map/dot_general | solution.py:45
  88.5 1.1 %fusion.20 = f32[3,768]{1,0:T(4,128)S(1)} fusion(f32[3,768]{1,0:T(4,128)S(1)} %fusion, s32[1024]{0:T(1024)S(1)} %bitcast.58, f32[1024]{0:T(1024)S(1)} %fusion.59, f32[6,1024]{1,0:T(8,128)S(1)} %fusion.16), kind=kOutput, calls=%fused_computation.24 | convolution fusion | flops 29103360 | bytes 46080 | tf_op jit(solution)/shard_map/dot_general | solution.py:45
  89.7 9.2 %collective-permute-start.9 = (f32[3,128]{1,0:T(4,128)S(1)}, f32[3,128]{1,0:T(4,128)S(1)}, u32[]{:S(2)}, u32[]{:S(2)}) collective-permute-start(f32[3,128]{1,0:T(4,128)S(1)} %get-tuple-element.3), channel_id=1, source_target_pairs={{0,1},{1,2},{2,3},{3,4},{4,5},{5,6},{6,7},{7,8},{8,9},{9,10},{10,1... | collective-permute-start | bytes 4616 | tf_op jit(solution)/shard_map/ppermute | solution.py:24
  98.9 1.9 %collective-permute-start.10 = (f32[3,128]{1,0:T(4,128)S(1)}, f32[3,128]{1,0:T(4,128)S(1)}, u32[]{:S(2)}, u32[]{:S(2)}) collective-permute-start(f32[3,128]{1,0:T(4,128)S(1)} %get-tuple-element.2), channel_id=1, source_target_pairs={{1,0},{2,1},{3,2},{4,3},{5,4},{6,5},{7,6},{8,7},{9,8},{10,9},{11,1... | collective-permute-start | bytes 4616 | tf_op jit(solution)/shard_map/ppermute | solution.py:25
  100.8 8.4 %collective-permute-done.10 = f32[3,128]{1,0:T(4,128)S(1)} collective-permute-done((f32[3,128]{1,0:T(4,128)S(1)}, f32[3,128]{1,0:T(4,128)S(1)}, u32[]{:S(2)}, u32[]{:S(2)}) %collective-permute-start.10) | collective-permute-done | bytes 1568 | tf_op jit(solution)/shard_map/ppermute | solution.py:25
  (46 shorter events, 11.4 us)
Async XLA Ops:
  2.6 14.0 %collective-permute-start = (f32[7,256]{1,0:T(8,128)S(1)}, f32[7,256]{1,0:T(8,128)S(1)}, u32[]{:S(2)}, u32[]{:S(2)}) collective-permute-start(f32[7,256]{1,0:T(8,128)S(1)} %fusion.30), channel_id=1, source_target_pairs={{0,256},{1,257},{2,258},{3,259},{4,260},{5,261},{6,262},{7,263},{8... | collective-permute-start | bytes 21512 | tf_op jit(solution)/shard_map/ppermute | solution.py:14
  18.0 9.0 %collective-permute-start.1 = (f32[7,256]{1,0:T(8,128)S(1)}, f32[7,256]{1,0:T(8,128)S(1)}, u32[]{:S(2)}, u32[]{:S(2)}) collective-permute-start(f32[7,256]{1,0:T(8,128)S(1)} %fusion.29), channel_id=1, source_target_pairs={{0,128},{1,129},{2,130},{3,131},{4,132},{5,133},{6,134},{7,135},{8... | collective-permute-start | bytes 21512 | tf_op jit(solution)/shard_map/ppermute | solution.py:14
  27.7 5.3 %collective-permute-start.2 = (f32[7,256]{1,0:T(8,128)S(1)}, f32[7,256]{1,0:T(8,128)S(1)}, u32[]{:S(2)}, u32[]{:S(2)}) collective-permute-start(f32[7,256]{1,0:T(8,128)S(1)} %fusion.27), channel_id=1, source_target_pairs={{0,64},{1,65},{2,66},{3,67},{4,68},{5,69},{6,70},{7,71},{8,72},{9,... | collective-permute-start | bytes 21512 | tf_op jit(solution)/shard_map/ppermute | solution.py:14
  34.2 18.9 %collective-permute-start.4 = (f32[6,128]{1,0:T(8,128)S(1)}, f32[6,128]{1,0:T(8,128)S(1)}, u32[]{:S(2)}, u32[]{:S(2)}) collective-permute-start(f32[6,128]{1,0:T(8,128)S(1)} %fusion.32), channel_id=1, source_target_pairs={{1,0},{2,1},{3,2},{4,3},{5,4},{6,5},{7,6},{8,7},{9,8},{10,9},{11,1... | collective-permute-start | bytes 9224 | tf_op jit(solution)/shard_map/ppermute | solution.py:25
  40.1 13.1 %collective-permute-start.3 = (f32[6,128]{1,0:T(8,128)S(1)}, f32[6,128]{1,0:T(8,128)S(1)}, u32[]{:S(2)}, u32[]{:S(2)}) collective-permute-start(f32[6,128]{1,0:T(8,128)S(1)} %fusion.32), channel_id=1, source_target_pairs={{0,1},{1,2},{2,3},{3,4},{4,5},{5,6},{6,7},{7,8},{8,9},{9,10},{10,1... | collective-permute-start | bytes 9224 | tf_op jit(solution)/shard_map/ppermute | solution.py:24
  51.2 20.3 %copy-start.2 = (s32[128]{0:T(128)S(1)}, s32[128]{0:T(128)}, u32[]{:S(2)}) copy-start(s32[128]{0:T(128)} %param.11) | copy-start | bytes 1540
  51.2 32.1 %copy-start = (f32[8,128,128]{2,1,0:T(8,128)S(1)}, f32[8,128,128]{2,1,0:T(8,128)}, u32[]{:S(2)}) copy-start(f32[8,128,128]{2,1,0:T(8,128)} %param.13) | copy-start | bytes 1572868
  58.7 4.5 %collective-permute-start.5 = (f32[3,128]{1,0:T(4,128)S(1)}, f32[3,128]{1,0:T(4,128)S(1)}, u32[]{:S(2)}, u32[]{:S(2)}) collective-permute-start(f32[3,128]{1,0:T(4,128)S(1)} %get-tuple-element.5), channel_id=1, source_target_pairs={{0,1},{1,2},{2,3},{3,4},{4,5},{5,6},{6,7},{7,8},{8,9},{9,10},{10,1... | collective-permute-start | bytes 4616 | tf_op jit(solution)/shard_map/ppermute | solution.py:24
  61.2 10.3 %collective-permute-start.6 = (f32[3,128]{1,0:T(4,128)S(1)}, f32[3,128]{1,0:T(4,128)S(1)}, u32[]{:S(2)}, u32[]{:S(2)}) collective-permute-start(f32[3,128]{1,0:T(4,128)S(1)} %get-tuple-element.4), channel_id=1, source_target_pairs={{1,0},{2,1},{3,2},{4,3},{5,4},{6,5},{7,6},{8,7},{9,8},{10,9},{11,1... | collective-permute-start | bytes 4616 | tf_op jit(solution)/shard_map/ppermute | solution.py:25
  72.0 12.2 %collective-permute-start.8 = (f32[3,128]{1,0:T(4,128)S(1)}, f32[3,128]{1,0:T(4,128)S(1)}, u32[]{:S(2)}, u32[]{:S(2)}) collective-permute-start(f32[3,128]{1,0:T(4,128)S(1)} %fusion.31), channel_id=1, source_target_pairs={{1,0},{2,1},{3,2},{4,3},{5,4},{6,5},{7,6},{8,7},{9,8},{10,9},{11,1... | collective-permute-start | bytes 4616 | tf_op jit(solution)/shard_map/ppermute | solution.py:25
  74.0 10.2 %collective-permute-start.7 = (f32[3,128]{1,0:T(4,128)S(1)}, f32[3,128]{1,0:T(4,128)S(1)}, u32[]{:S(2)}, u32[]{:S(2)}) collective-permute-start(f32[3,128]{1,0:T(4,128)S(1)} %fusion.31), channel_id=1, source_target_pairs={{0,1},{1,2},{2,3},{3,4},{4,5},{5,6},{6,7},{7,8},{8,9},{9,10},{10,1... | collective-permute-start | bytes 4616 | tf_op jit(solution)/shard_map/ppermute | solution.py:24
  87.4 22.7 %copy-start.1 = (f32[1024]{0:T(1024)}, f32[1024]{0:T(1024)S(1)}, u32[]{:S(2)}) copy-start(f32[1024]{0:T(1024)S(1)} %fusion.59) | copy-start | bytes 12292
  89.7 11.1 %collective-permute-start.9 = (f32[3,128]{1,0:T(4,128)S(1)}, f32[3,128]{1,0:T(4,128)S(1)}, u32[]{:S(2)}, u32[]{:S(2)}) collective-permute-start(f32[3,128]{1,0:T(4,128)S(1)} %get-tuple-element.3), channel_id=1, source_target_pairs={{0,1},{1,2},{2,3},{3,4},{4,5},{5,6},{6,7},{7,8},{8,9},{9,10},{10,1... | collective-permute-start | bytes 4616 | tf_op jit(solution)/shard_map/ppermute | solution.py:24
  98.9 10.3 %collective-permute-start.10 = (f32[3,128]{1,0:T(4,128)S(1)}, f32[3,128]{1,0:T(4,128)S(1)}, u32[]{:S(2)}, u32[]{:S(2)}) collective-permute-start(f32[3,128]{1,0:T(4,128)S(1)} %get-tuple-element.2), channel_id=1, source_target_pairs={{1,0},{2,1},{3,2},{4,3},{5,4},{6,5},{7,6},{8,7},{9,8},{10,9},{11,1... | collective-permute-start | bytes 4616 | tf_op jit(solution)/shard_map/ppermute | solution.py:25
where the time goes:
time: 111 us; the launch traced here: 110 us
  starting transfers between devices  61 us (55%)
  waiting for transfers between devices  19.4 us (17%)
  matrix products  17.6 us (16%)
  local copies, waits for them, and re-layouts  9.54 us (9%)
  other arithmetic  1.73 us (2%)
    ppermute x4, starting transfers between devices, with_halo(): before = lax.ppermute(last, axis, up)  26.2 us
    ppermute x3, starting transfers between devices, partner(): return lax.ppermute(value, axis, pairs)  23.1 us
    ppermute x4, waiting for transfers between devices, with_halo(): after = lax.ppermute(first, axis, down)  16.7 us
    ppermute x4, starting transfers between devices, with_halo(): after = lax.ppermute(first, axis, down)  11.6 us
    dot_general x9, matrix products, pick(): lax.dot_general(field, table, (((1,), (1,)), ((), ())), precision=lax.Pre...  9.26 us
    dot_general x9, matrix products, spread(): jnp.dot(values, table, precision=lax.Precision.HIGHEST, preferred_element...  7.39 us
    unnamed x7, local copies, waits for them, and re-layouts  5.87 us
    ppermute x3, waiting for transfers between devices, partner(): return lax.ppermute(value, axis, pairs)  2.66 us
  transfers between devices with their start and end apart: 11, of which 4 were waited for; matrix products, arithmetic and copies ran while one was open for 10% of the time, Pallas kernels for 0%

commit v1 on v0

v1 whole, which is shorter than its diff:
```python
import jax
import jax.numpy as jnp
from jax import lax
from jax.experimental import pallas as pl
from jax.experimental.pallas import tpu as pltpu
from jax.sharding import PartitionSpec as P

MESH = pl.DeviceIdType.MESH
F32 = jnp.float32
BF16 = jnp.bfloat16
MESSAGES = 15


def split(x):
    head = x.astype(BF16).astype(F32)
    return jnp.concatenate([head, x - head], axis=0).astype(BF16)


def join(y):
    half = y.shape[0] // 2
    return y[:half] + y[half:]


def pick(x, table):
    return join(jnp.dot(split(x), table, preferred_element_type=F32))


def spread(x, table):
    return join(
        lax.dot_general(split(x), table, (((1,), (1,)), ((), ())), preferred_element_type=F32)
    )


def rows8(*pieces):
    have = sum(piece.shape[0] for piece in pieces)
    if have < 8:
        pieces += (jnp.zeros((8 - have, pieces[0].shape[1]), F32),)
    return jnp.concatenate(pieces, axis=0)


def put_one_hot(table, row, base=0):
    extent, width = table.shape
    block = 64

    def step(i, carry):
        slot = lax.broadcasted_iota(jnp.int32, (block, width), 0) + (i * block + base)
        table[pl.ds(pl.multiple_of(i * block, block), block), :] = jnp.where(
            slot == row, 1.0, 0.0
        ).astype(BF16)
        return carry

    lax.fori_loop(0, extent // block, step, 0)


def kernel(
    count,
    pos_hbm, vel_hbm, mass_hbm, lists_hbm, rim_hbm, pair_hbm, tiles_hbm,
    vel_out, lam_out,
    pos_in, vel_in, mass_in, lists_in, rim_in, pair_in, tiles_in,
    ends, swap_tab, peer_tab, rim_tab, rimq_tab, code_tab, tiles_hi, tiles_lo,
    send_a, send_k, send_m, send_b1, send_b2, send_b3, send_c, send_f,
    recv_a, recv_k, recv_m, recv_b1, recv_b2, recv_b3, recv_c, recv_f,
    in_sem, send_sem, recv_sem,
):
    grains = pos_in.shape[1]
    width = rim_in.shape[1]
    contacts = pair_in.shape[1]
    tiles, tile = tiles_in.shape[:2]
    bits = count.bit_length() - 1
    far, mid, near = (1 << (bits - 1 - level) for level in range(3))
    me = lax.axis_index("parts")

    def shifted(base, by):
        return lax.rem(base + (by + count), count)

    def flipped(base, mask):
        return lax.bitwise_xor(base, jnp.int32(mask))

    loads = [
        pltpu.make_async_copy(src, dst, in_sem.at[i])
        for i, (src, dst) in enumerate(
            [
                (lists_hbm, lists_in), (pos_hbm, pos_in), (vel_hbm, vel_in), (mass_hbm, mass_in),
                (rim_hbm, rim_in), (pair_hbm, pair_in), (tiles_hbm, tiles_in),
            ]
        )
    ]
    for load in loads:
        load.start()

    barrier = pltpu.get_barrier_semaphore()
    senders = [
        flipped(me, far), flipped(me, far | mid), flipped(me, mid), flipped(me, near),
        shifted(me, -1), shifted(me, 1),
        flipped(shifted(me, -1), near), flipped(shifted(me, 1), near),
        shifted(me, -2), shifted(me, 2),
    ]
    for sender in senders:
        pl.semaphore_signal(barrier, inc=1, device_id=(sender,), device_id_type=MESH)

    twin = flipped(me, near)
    routes = [
        (send_a, recv_a.at[0], flipped(me, far)),
        (send_a, recv_a.at[1], flipped(me, far | mid)),
        (send_k, recv_k, flipped(me, mid)),
        (send_m, recv_m, twin),
        (send_b1, recv_b1, twin),
        (send_b2, recv_b2.at[0], shifted(me, 1)),
        (send_b2, recv_b2.at[1], shifted(me, -1)),
        (send_b3, recv_b3.at[0], shifted(twin, 1)),
        (send_b3, recv_b3.at[1], shifted(twin, -1)),
        (send_c.at[0], recv_c.at[0], shifted(me, 1)),
        (send_c.at[1], recv_c.at[1], shifted(me, -1)),
        (send_c.at[0], recv_c.at[2], shifted(me, 2)),
        (send_c.at[1], recv_c.at[3], shifted(me, -2)),
        (send_f.at[0], recv_f.at[0], shifted(me, 1)),
        (send_f.at[1], recv_f.at[1], shifted(me, -1)),
    ]
    copies = [
        pltpu.make_async_remote_copy(
            src_ref=src, dst_ref=dst, send_sem=send_sem.at[i], recv_sem=recv_sem.at[i],
            device_id=(target,), device_id_type=MESH,
        )
        for i, (src, dst, target) in enumerate(routes)
    ]

    for load in loads[:5]:
        load.wait()
    swap = [swap_tab.at[level] for level in range(3)]
    for level in range(3):
        put_one_hot(swap[level], lists_in[level : level + 1, :])
    put_one_hot(rim_tab, rim_in[...])
    ones = jnp.ones((8, lists_in.shape[1]), F32)
    keep = [1.0 - spread(ones, swap[level][...])[:1] for level in range(3)]
    state = rows8(pos_in[...], vel_in[...], mass_in[...])
    lists = lists_in[...].astype(F32)
    kept = state * keep[0]
    send_a[...] = pick(state, swap[0][...])
    send_k[...] = jnp.concatenate(
        [kept[:7], jnp.concatenate([lists[0:1], lists[1:2]], axis=1)], axis=0
    )
    order = lax.broadcasted_iota(jnp.int32, (8, lists_in.shape[1]), 1).astype(F32) + 1.0
    rim_code = pick(spread(order, swap[2][...]), rim_tab[...])
    send_m[...] = rim_code
    rim_keep = jnp.where(rim_code[:1] < 0.5, 1.0, 0.0)

    pl.semaphore_wait(barrier, len(senders))
    for i in (0, 1, 2, 3):
        copies[i].start()

    loads[5].wait()
    first, second = pair_in[0:1, :], pair_in[1:2, :]

    def put_ends(i, carry):
        slot = lax.broadcasted_iota(jnp.int32, (32, contacts), 0) + i * 32
        ends[pl.ds(pl.multiple_of(i * 32, 32), 32), :] = (
            jnp.where(slot == first, 1.0, 0.0) - jnp.where(slot == second, 1.0, 0.0)
        ).astype(BF16)
        return carry

    lax.fori_loop(0, ends.shape[0] // 32, put_ends, 0)

    loads[6].wait()
    eye = lax.broadcasted_iota(jnp.int32, (tile, tile), 0) == lax.broadcasted_iota(
        jnp.int32, (tile, tile), 1
    )
    diags = []
    for t in range(tiles):
        block = tiles_in[t]
        head = block.astype(BF16)
        tiles_hi[t * tile : (t + 1) * tile, :] = head
        tiles_lo[t * tile : (t + 1) * tile, :] = (block - head.astype(F32)).astype(BF16)
        diags.append(jnp.sum(jnp.where(eye, block, 0.0), axis=0, keepdims=True))
    diag = jnp.concatenate(diags, axis=1)
    own_tile = lax.broadcasted_iota(jnp.int32, (tiles, contacts), 0) == (
        lax.broadcasted_iota(jnp.int32, (tiles, contacts), 1) // tile
    )

    def coupled(lam):
        table = jnp.concatenate(
            [lam[:, t * tile : (t + 1) * tile] for t in range(tiles)], axis=0
        )
        product = spread(table, tiles_hi[...]) + spread(table, tiles_lo[...])
        return jnp.sum(jnp.where(own_tile, product, 0.0), axis=0, keepdims=True)

    lam = jnp.zeros((1, contacts), F32)
    pull = coupled(lam)

    copies[3].wait_recv()
    put_one_hot(code_tab, recv_m[0:1, :].astype(jnp.int32), 1)
    rimq_tab[...] = jnp.dot(swap[2][...], code_tab[...], preferred_element_type=F32).astype(BF16)

    copies[2].wait_recv()
    peer_lists = recv_k[7:8, :].astype(jnp.int32)
    half = lists_in.shape[1]
    put_one_hot(peer_tab.at[0], peer_lists[:, :half])
    put_one_hot(peer_tab.at[1], peer_lists[:, half:])
    peer_kept = rows8(recv_k[0:7, :])

    copies[1].wait_recv()
    peer = peer_kept + spread(recv_a[1], peer_tab[0])
    crossing = pick(peer, peer_tab[1])
    copies[0].wait_recv()
    state = kept + spread(recv_a[0], swap[0][...])
    state = state * keep[1] + spread(crossing, swap[1][...])

    own_rim = pick(state, rim_tab[...]) * rim_keep
    send_b3[...] = pick(state, rimq_tab[...])
    send_b2[...] = own_rim
    for i in (7, 8, 5, 6):
        copies[i].start()
    send_b1[...] = pick(state, swap[2][...])
    copies[4].start()

    state = state * keep[2]
    copies[4].wait_recv()
    state = state + spread(recv_b1[...], swap[2][...])
    for i in (5, 6, 7, 8):
        copies[i].wait_recv()
    left = jnp.where(me >= 1, recv_b2[0] + recv_b3[0], 0.0)
    right = jnp.where(me <= count - 2, recv_b2[1] + recv_b3[1], 0.0)
    gathered = pick(jnp.concatenate([state, left, right], axis=1), ends[...])
    normal = gathered[0:3]
    relative = gathered[3:6]
    vel, mass = state[3:6], state[6:7]

    speed = jnp.sum(normal * relative, axis=0, keepdims=True)
    lam = jnp.maximum(0.0, lam - (pull + speed) / diag)
    partial = spread(rows8(normal * lam), ends[...])
    local = partial[0:3, :grains]
    ghost_left = partial[0:3, grains : grains + width]
    ghost_right = partial[0:3, grains + width :]
    at_rim = pick(partial[:, :grains], rim_tab[...])[0:3]
    send_c[0] = rows8(ghost_right, at_rim)
    send_c[1] = rows8(ghost_left, at_rim)
    for i in (9, 10, 11, 12):
        copies[i].start()
    pull = coupled(lam)
    for i in (9, 10, 11, 12):
        copies[i].wait_recv()
    zero = jnp.zeros((3, width), F32)
    incoming = jnp.where(me >= 1, recv_c[0, 0:3], zero) + jnp.where(
        me <= count - 2, recv_c[1, 0:3], zero
    )
    current = vel + mass * (local + spread(rows8(incoming), rim_tab[...])[0:3])
    total_left = recv_c[0, 3:6] + ghost_left + jnp.where(me >= 2, recv_c[2, 0:3], zero)
    total_right = recv_c[1, 3:6] + ghost_right + jnp.where(me <= count - 3, recv_c[3, 0:3], zero)
    fresh_left = left[3:6] + left[6:7] * total_left
    fresh_right = right[3:6] + right[6:7] * total_right
    relative = pick(
        rows8(jnp.concatenate([current, fresh_left, fresh_right], axis=1)), ends[...]
    )[0:3]

    speed = jnp.sum(normal * relative, axis=0, keepdims=True)
    lam = jnp.maximum(0.0, lam - (pull + speed) / diag)
    partial = spread(rows8(normal * lam), ends[...])
    send_f[0] = rows8(partial[0:3, grains + width :])
    send_f[1] = rows8(partial[0:3, grains : grains + width])
    for i in (13, 14):
        copies[i].start()
    lam_out[...] = lam
    local = partial[0:3, :grains]
    for i in (13, 14):
        copies[i].wait_recv()
    incoming = jnp.where(me >= 1, recv_f[0, 0:3], zero) + jnp.where(
        me <= count - 2, recv_f[1, 0:3], zero
    )
    vel_out[...] = vel + mass * (local + spread(rows8(incoming), rim_tab[...])[0:3])
    for copy in copies:
        copy.wait_send()


def body(count, positions, velocity, inv_mass, swap_lists, rim_list, contact_pair, delassus):
    grains = positions.shape[1]
    half = swap_lists.shape[1]
    width = rim_list.shape[0]
    contacts = contact_pair.shape[1]
    tiles, tile = delassus.shape[:2]
    args = (
        positions, velocity, inv_mass.reshape(1, grains), swap_lists, rim_list.reshape(1, width),
        contact_pair, delassus,
    )

    def grid(rows, columns):
        return pltpu.VMEM((rows, columns), F32)

    current, lam = pl.pallas_call(
        lambda *refs: kernel(count, *refs),
        out_shape=(
            jax.ShapeDtypeStruct((3, grains), F32),
            jax.ShapeDtypeStruct((1, contacts), F32),
        ),
        in_specs=[pl.BlockSpec(memory_space=pltpu.HBM)] * len(args),
        out_specs=(
            pl.BlockSpec(memory_space=pltpu.VMEM),
            pl.BlockSpec(memory_space=pltpu.VMEM),
        ),
        scratch_shapes=[pltpu.VMEM(arg.shape, arg.dtype) for arg in args]
        + [
            pltpu.VMEM((grains + 2 * width, contacts), BF16),
            pltpu.VMEM((3, grains, half), BF16),
            pltpu.VMEM((2, grains, half), BF16),
            pltpu.VMEM((grains, width), BF16),
            pltpu.VMEM((grains, width), BF16),
            pltpu.VMEM((half, width), BF16),
            pltpu.VMEM((contacts, tile), BF16),
            pltpu.VMEM((contacts, tile), BF16),
            grid(8, half), grid(8, grains), grid(8, width),
            grid(8, half), grid(8, width), grid(8, width),
            pltpu.VMEM((2, 8, width), F32), pltpu.VMEM((2, 8, width), F32),
            pltpu.VMEM((2, 8, half), F32), grid(8, grains), grid(8, width),
            grid(8, half), pltpu.VMEM((2, 8, width), F32), pltpu.VMEM((2, 8, width), F32),
            pltpu.VMEM((4, 8, width), F32), pltpu.VMEM((2, 8, width), F32),
            pltpu.SemaphoreType.DMA((len(args),)),
            pltpu.SemaphoreType.DMA((MESSAGES,)),
            pltpu.SemaphoreType.DMA((MESSAGES,)),
        ],
        compiler_params=pltpu.CompilerParams(
            collective_id=0, has_side_effects=True, vmem_limit_bytes=32 << 20
        ),
        name="contact_step",
    )(*args)
    return current, lam.reshape(contacts)


def solution(mesh):
    count = mesh.shape["parts"]
    in_specs = (
        P(None, "parts"),
        P(None, "parts"),
        P("parts"),
        P(None, "parts"),
        P("parts"),
        P(None, "parts"),
        P("parts", None, None),
    )
    out_specs = (P(None, "parts"), P("parts"))
    return jax.shard_map(
        lambda *args: body(count, *args),
        mesh=mesh, in_specs=in_specs, out_specs=out_specs, check_vma=False,
    )
```

time: 111 us -> 44.3 us (0.40)
  the two profiles are of different devices: /device:TPU:127 before, /device:TPU:1 now
where the time goes in v1:
time: 44.3 us; the launch traced here: 44 us
  Pallas kernels  37.6 us (85%)
  local copies, waits for them, and re-layouts  5.68 us (13%)
  between operations  0.66 us (1%)
    pallas_call x1, Pallas kernels, body(): pl.pallas_call(lambda *refs: kernel(count, *refs), out_shape=(jax.ShapeDt...  37.6 us
    unnamed x16, local copies, waits for them, and re-layouts  5.68 us

profile of v1, /device:TPU:1, one launch (start us, length us, event | category | flops | bytes accessed | tf_op | source)
XLA Modules:
  0.0 44.0 jit_solution(1019250015411974765)
XLA Ops:
  0.6 0.0 copy-start.5
  0.6 0.0 copy-start.6
  0.7 0.7 %copy-done.5 = f32[512]{0:T(512)S(1)} copy-done((f32[512]{0:T(512)S(1)}, f32[512]{0:T(512)}, u32[]{:S(2)}) %copy-start.5) | copy-done | bytes 2072
  1.3 0.0 copy-done.6
  1.3 0.0 copy-start
  1.3 1.0 %copy-done = f32[8,128,128]{2,1,0:T(8,128)S(1)} copy-done((f32[8,128,128]{2,1,0:T(8,128)S(1)}, f32[8,128,128]{2,1,0:T(8,128)}, u32[]{:S(2)}) %copy-start) | copy-done | bytes 524312
  2.4 0.0 copy-start.1
  2.4 0.7 %copy-done.1 = f32[3,512]{1,0:T(4,128)S(1)} copy-done((f32[3,512]{1,0:T(4,128)S(1)}, f32[3,512]{1,0:T(4,128)}, u32[]{:S(2)}) %copy-start.1) | copy-done | bytes 6168
  3.1 0.0 copy-start.2
  3.1 0.7 %copy-done.2 = f32[3,512]{1,0:T(4,128)S(1)} copy-done((f32[3,512]{1,0:T(4,128)S(1)}, f32[3,512]{1,0:T(4,128)}, u32[]{:S(2)}) %copy-start.2) | copy-done | bytes 6168
  3.8 0.0 copy-start.3
  3.8 0.7 %copy-done.3 = s32[2,1024]{1,0:T(2,128)S(1)} copy-done((s32[2,1024]{1,0:T(2,128)S(1)}, s32[2,1024]{1,0:T(2,128)}, u32[]{:S(2)}) %copy-start.3) | copy-done | bytes 8216
  4.5 0.0 copy-start.4
  4.5 0.7 %copy-done.4 = s32[3,256]{1,0:T(4,128)S(1)} copy-done((s32[3,256]{1,0:T(4,128)S(1)}, s32[3,256]{1,0:T(4,128)}, u32[]{:S(2)}) %copy-start.4) | copy-done | bytes 3096
  5.1 37.6 %contact_step.1 = (f32[3,512]{1,0:T(4,128)S(1)}, f32[1,1024]{1,0:T(1,128)S(1)}) custom-call(f32[3,512]{1,0:T(4,128)S(1)} %copy-done.1, f32[3,512]{1,0:T(4,128)S(1)} %copy-done.2, f32[1,512]{1,0:T(1,128)S(1)} %bitcast.4, s32[3,256]{1,0:T(4,128)S(1)} %copy-done.4, s32[1,128]{1,0:T(1,128)S(1)} %bitcast.5, s32[2,1024]{1,0:T(2,128)S(1)} %copy-done.3, ...), custom_call_target="tpu_custom_call" | custom-call | tf_op jit(solution)/shard_map/contact_step/pallas_call | solution.py:287
  42.8 0.6 %copy.11 = f32[3,512]{1,0:T(4,128)} copy(f32[3,512]{1,0:T(4,128)S(1)} %get-tuple-element.8) | data formatting | bytes 12288
  43.4 0.6 %copy.12 = f32[1024]{0:T(1024)} copy(f32[1024]{0:T(1024)S(1)} %bitcast.3) | data formatting | bytes 8192
Async XLA Ops:
  0.6 0.7 %copy-start.5 = (f32[512]{0:T(512)S(1)}, f32[512]{0:T(512)}, u32[]{:S(2)}) copy-start(f32[512]{0:T(512)} %param.9) | copy-start | bytes 6148
  0.6 0.7 %copy-start.6 = (s32[128]{0:T(128)S(1)}, s32[128]{0:T(128)}, u32[]{:S(2)}) copy-start(s32[128]{0:T(128)} %param.11) | copy-start | bytes 1540
  1.3 1.0 %copy-start = (f32[8,128,128]{2,1,0:T(8,128)S(1)}, f32[8,128,128]{2,1,0:T(8,128)}, u32[]{:S(2)}) copy-start(f32[8,128,128]{2,1,0:T(8,128)} %refs_6_.1) | copy-start | bytes 1572868
  2.4 0.7 %copy-start.1 = (f32[3,512]{1,0:T(4,128)S(1)}, f32[3,512]{1,0:T(4,128)}, u32[]{:S(2)}) copy-start(f32[3,512]{1,0:T(4,128)} %refs_0_.1) | copy-start | bytes 18436
  3.1 0.7 %copy-start.2 = (f32[3,512]{1,0:T(4,128)S(1)}, f32[3,512]{1,0:T(4,128)}, u32[]{:S(2)}) copy-start(f32[3,512]{1,0:T(4,128)} %refs_1_.1) | copy-start | bytes 18436
  3.8 0.7 %copy-start.3 = (s32[2,1024]{1,0:T(2,128)S(1)}, s32[2,1024]{1,0:T(2,128)}, u32[]{:S(2)}) copy-start(s32[2,1024]{1,0:T(2,128)} %refs_5_.1) | copy-start | bytes 24580
  4.5 0.7 %copy-start.4 = (s32[3,256]{1,0:T(4,128)S(1)}, s32[3,256]{1,0:T(4,128)}, u32[]{:S(2)}) copy-start(s32[3,256]{1,0:T(4,128)} %refs_3_.1) | copy-start | bytes 9220

commit v2 on v1

v2 whole, which is shorter than its diff:
```python
import functools

import jax
import jax.numpy as jnp
from jax import lax
from jax.experimental import pallas as pl
from jax.experimental.pallas import tpu as pltpu
from jax.sharding import PartitionSpec as P

MESH = pl.DeviceIdType.MESH
F32 = jnp.float32
BF16 = jnp.bfloat16
MESSAGES = 18


def split(x):
    head = x.astype(BF16).astype(F32)
    return jnp.concatenate([head, x - head], axis=0).astype(BF16)


def join(y):
    half = y.shape[0] // 2
    return y[:half] + y[half:]


def pick(x, table):
    return join(jnp.dot(split(x), table, preferred_element_type=F32))


def spread(x, table):
    return join(
        lax.dot_general(split(x), table, (((1,), (1,)), ((), ())), preferred_element_type=F32)
    )


def rows8(*pieces):
    have = sum(piece.shape[0] for piece in pieces)
    if have < 8:
        pieces += (jnp.zeros((8 - have, pieces[0].shape[1]), F32),)
    return jnp.concatenate(pieces, axis=0)


def put_one_hot(table, row, base=0):
    extent, width = table.shape
    block = 64

    def step(i, carry):
        slot = lax.broadcasted_iota(jnp.int32, (block, width), 0) + (i * block + base)
        table[pl.ds(pl.multiple_of(i * block, block), block), :] = jnp.where(
            slot == row, 1.0, 0.0
        ).astype(BF16)
        return carry

    lax.fori_loop(0, extent // block, step, 0)


def kernel(
    count,
    pos_hbm, vel_hbm, mass_hbm, lists_hbm, rim_hbm, pair_hbm, tiles_hbm,
    vel_out, lam_out,
    pos_in, vel_in, mass_in, lists_in, rim_in, pair_in, tiles_in,
    ends, tab0, tab1, tab2, rim_tab, slot_tab, edge_tab, tiles_hi, tiles_lo,
    send_a, send_k, send_r, send_c, send_f,
    recv_a, recv_l, recv_k, recv_r, recv_c, recv_f,
    in_sem, send_sem, recv_sem,
):
    grains = pos_in.shape[1]
    half = lists_in.shape[1]
    width = rim_in.shape[1]
    contacts = pair_in.shape[1]
    tiles, tile = tiles_in.shape[:2]
    bits = count.bit_length() - 1
    far, mid, near = (1 << (bits - 1 - level) for level in range(3))
    masks = (0, near, mid, mid | near)
    me = lax.axis_index("parts")
    high = me >= far
    low = me < far

    def shifted(base, by):
        return lax.rem(base + (by + count), count)

    def flipped(base, mask):
        return lax.bitwise_xor(base, jnp.int32(mask))

    def inside(by):
        return me >= -by if by < 0 else me < count - by

    loads = [
        pltpu.make_async_copy(src, dst, in_sem.at[i])
        for i, (src, dst) in enumerate(
            [
                (lists_hbm, lists_in), (pos_hbm, pos_in), (vel_hbm, vel_in), (mass_hbm, mass_in),
                (rim_hbm, rim_in), (pair_hbm, pair_in), (tiles_hbm, tiles_in),
            ]
        )
    ]
    for load in loads:
        load.start()

    barrier = pltpu.get_barrier_semaphore()

    def greet(peer):
        pl.semaphore_signal(barrier, inc=1, device_id=(peer,), device_id_type=MESH)

    @pl.when(low)
    def _():
        for mask in masks:
            greet(flipped(me, far | mask))

    for mask in masks[1:]:
        greet(flipped(me, mask))
    awaited = 3 + 4 * high.astype(jnp.int32)
    for by in (1, -1, 2, -2):
        pl.when(inside(by))(functools.partial(greet, shifted(me, by)))
        awaited += inside(by).astype(jnp.int32)

    routes = [(send_a, recv_a.at[k], flipped(me, far | masks[k]), 0) for k in range(4)]
    routes += [(lists_in, recv_l.at[k - 1], flipped(me, masks[k]), 0) for k in (1, 2, 3)]
    routes += [(send_k, recv_k.at[k - 1], flipped(me, masks[k]), 0) for k in (1, 2, 3)]
    routes += [
        (send_r, recv_r.at[0], shifted(me, 1), 1),
        (send_r, recv_r.at[1], shifted(me, -1), -1),
        (send_c.at[0], recv_c.at[0], shifted(me, 1), 1),
        (send_c.at[1], recv_c.at[1], shifted(me, -1), -1),
        (send_c.at[0], recv_c.at[2], shifted(me, 2), 2),
        (send_c.at[1], recv_c.at[3], shifted(me, -2), -2),
        (send_f.at[0], recv_f.at[0], shifted(me, 1), 1),
        (send_f.at[1], recv_f.at[1], shifted(me, -1), -1),
    ]
    copies = [
        pltpu.make_async_remote_copy(
            src_ref=src, dst_ref=dst, send_sem=send_sem.at[i], recv_sem=recv_sem.at[i],
            device_id=(target,), device_id_type=MESH,
        )
        for i, (src, dst, target, _) in enumerate(routes)
    ]

    def guarded(action, by):
        if by == 0:
            action()
        else:
            pl.when(inside(by))(action)

    def send(*which):
        for i in which:
            guarded(copies[i].start, routes[i][3])

    def receive(*which):
        for i in which:
            guarded(copies[i].wait_recv, -routes[i][3])

    def blank(*refs):
        for ref in refs:
            ref[...] = jnp.zeros(ref.shape, F32)

    for load in loads[:4]:
        load.wait()
    put_one_hot(tab0.at[0], lists_in[0:1, :])
    state = rows8(pos_in[...], vel_in[...], mass_in[...])
    send_a[...] = pick(state, tab0[0])

    pl.semaphore_wait(barrier, awaited)
    pl.when(high)(lambda: send(0, 1, 2, 3))
    send(4, 5, 6)
    ones = jnp.ones((8, half), F32)

    def keep(table):
        return 1.0 - spread(ones, table)[:1]

    kept = state * keep(tab0[0])
    send_k[...] = kept
    send(7, 8, 9)

    pl.when(me < 1)(lambda: blank(recv_r.at[0], recv_c.at[0], recv_f.at[0]))
    pl.when(me > count - 2)(lambda: blank(recv_r.at[1], recv_c.at[1], recv_f.at[1]))
    pl.when(me < 2)(lambda: blank(recv_c.at[2]))
    pl.when(me > count - 3)(lambda: blank(recv_c.at[3]))

    loads[4].wait()
    loads[5].wait()
    rim_row = rim_in[...]
    put_one_hot(tab1.at[0], lists_in[1:2, :])
    put_one_hot(tab2.at[0], lists_in[2:3, :])
    put_one_hot(rim_tab, rim_row)
    first, second = pair_in[0:1, :], pair_in[1:2, :]

    def touch(slot):
        return (jnp.where(slot == first, 1.0, 0.0) - jnp.where(slot == second, 1.0, 0.0)).astype(
            BF16
        )

    def put_ends(i, carry):
        slot = lax.broadcasted_iota(jnp.int32, (32, contacts), 0) + i * 32
        ends[pl.ds(pl.multiple_of(i * 32, 32), 32), :] = touch(slot)
        return carry

    extent = grains + 2 * width
    lax.fori_loop(0, extent // 32, put_ends, 0)
    across = lax.broadcasted_iota(jnp.int32, (width, width), 0) == lax.broadcasted_iota(
        jnp.int32, (width, width), 1
    )
    rim_column = jnp.sum(jnp.where(across, rim_row, 0), axis=1, keepdims=True)
    for i in range(0, width, 32):
        ends[extent + i : extent + i + 32, :] = touch(rim_column[i : i + 32])

    loads[6].wait()
    eye = lax.broadcasted_iota(jnp.int32, (tile, tile), 0) == lax.broadcasted_iota(
        jnp.int32, (tile, tile), 1
    )
    diags = []
    for t in range(tiles):
        block = tiles_in[t]
        head = block.astype(BF16)
        tiles_hi[t * tile : (t + 1) * tile, :] = head
        tiles_lo[t * tile : (t + 1) * tile, :] = (block - head.astype(F32)).astype(BF16)
        diags.append(jnp.sum(jnp.where(eye, block, 0.0), axis=0, keepdims=True))
    diag = jnp.concatenate(diags, axis=1)
    own_tile = lax.broadcasted_iota(jnp.int32, (tiles, contacts), 0) == (
        lax.broadcasted_iota(jnp.int32, (tiles, contacts), 1) // tile
    )

    def coupled(lam):
        table = jnp.concatenate(
            [lam[:, t * tile : (t + 1) * tile] for t in range(tiles)], axis=0
        )
        product = spread(table, tiles_hi[...]) + spread(table, tiles_lo[...])
        return jnp.sum(jnp.where(own_tile, product, 0.0), axis=0, keepdims=True)

    lam = jnp.zeros((1, contacts), F32)
    pull = coupled(lam)

    code_row = lax.broadcasted_iota(jnp.int32, (8, half), 0)
    order = lax.broadcasted_iota(jnp.int32, (8, half), 1).astype(F32) + 1.0

    def coded(k, rows):
        codes = spread(jnp.where(code_row == k, order, 0.0), tab0[k])
        return jnp.concatenate([rows, codes], axis=0)

    parts = [coded(0, kept)]
    for k in (1, 2, 3):
        receive(3 + k)
        put_one_hot(tab0.at[k], recv_l[k - 1, 0:1, :])
        put_one_hot(tab1.at[k], recv_l[k - 1, 1:2, :])
        if k == 1:
            put_one_hot(tab2.at[1], recv_l[0, 2:3, :])
        receive(6 + k)
        parts.append(coded(k, recv_k[k - 1]))
    pair = [
        parts[k] * keep(tab1[k]) + spread(pick(parts[k + 2], tab1[k + 2]), tab1[k])
        for k in (0, 1)
    ]
    state = pair[0] * keep(tab2[0]) + spread(pick(pair[1], tab2[1]), tab2[0])
    edge = pick(state, rim_tab[...])
    for k in range(4):
        put_one_hot(
            edge_tab.at[k * half : (k + 1) * half, :], edge[8 + k : 9 + k].astype(jnp.int32), 1
        )
        put_one_hot(
            slot_tab.at[k * half : (k + 1) * half, :], state[8 + k : 9 + k].astype(jnp.int32), 1
        )

    @pl.when(low)
    def _():
        for k in (2, 3, 1, 0):
            receive(k)
            send(k)

    pl.when(high)(lambda: receive(2, 3, 1, 0))
    arrived = split(jnp.concatenate([recv_a[k] for k in range(4)], axis=1))
    edge = edge[:8] + join(jnp.dot(arrived, edge_tab[...], preferred_element_type=F32))
    send_r[...] = edge
    send(10, 11)
    state = state[:8] + join(jnp.dot(arrived, slot_tab[...], preferred_element_type=F32))
    vel, mass = state[3:6], state[6:7]
    gathered = pick(state, ends[:grains, :])

    receive(10, 11)
    left, right = recv_r[0], recv_r[1]
    gathered += pick(jnp.concatenate([left, right], axis=1), ends[grains:extent, :])
    normal = gathered[0:3]
    speed = jnp.sum(normal * gathered[3:6], axis=0, keepdims=True)
    lam = jnp.maximum(0.0, lam - (pull + speed) / diag)
    force = rows8(normal * lam)
    partial = spread(force, ends[grains:, :])[0:3]
    ghost_left, ghost_right = partial[:, :width], partial[:, width : 2 * width]
    at_rim = partial[:, 2 * width :]
    send_c[0] = rows8(ghost_right, at_rim)
    send_c[1] = rows8(ghost_left, at_rim)
    send(12, 13, 14, 15)
    local = spread(force, ends[:grains, :])[0:3]
    base = pick(rows8(vel + mass * local), ends[:grains, :])[0:3]
    pull = coupled(lam)

    receive(12, 13, 14, 15)
    incoming = edge[6:7] * (recv_c[0, 0:3] + recv_c[1, 0:3])
    fresh_left = left[3:6] + left[6:7] * (recv_c[0, 3:6] + ghost_left + recv_c[2, 0:3])
    fresh_right = right[3:6] + right[6:7] * (recv_c[1, 3:6] + ghost_right + recv_c[3, 0:3])
    relative = base + pick(
        rows8(jnp.concatenate([fresh_left, fresh_right, incoming], axis=1)), ends[grains:, :]
    )[0:3]
    speed = jnp.sum(normal * relative, axis=0, keepdims=True)
    lam = jnp.maximum(0.0, lam - (pull + speed) / diag)
    force = rows8(normal * lam)
    partial = spread(force, ends[grains:extent, :])
    send_f[0] = partial[:, width:]
    send_f[1] = partial[:, :width]
    send(16, 17)
    lam_out[...] = lam
    base = vel + mass * spread(force, ends[:grains, :])[0:3]

    receive(16, 17)
    vel_out[...] = base + mass * spread(recv_f[0] + recv_f[1], rim_tab[...])[0:3]
    for i in range(MESSAGES):
        guarded(copies[i].wait_send, routes[i][3])


def body(count, positions, velocity, inv_mass, swap_lists, rim_list, contact_pair, delassus):
    grains = positions.shape[1]
    half = swap_lists.shape[1]
    width = rim_list.shape[0]
    contacts = contact_pair.shape[1]
    tiles, tile = delassus.shape[:2]
    args = (
        positions, velocity, inv_mass.reshape(1, grains), swap_lists, rim_list.reshape(1, width),
        contact_pair, delassus,
    )
    args = tuple(pltpu.with_memory_space_constraint(arg, pltpu.HBM) for arg in args)

    current, lam = pl.pallas_call(
        lambda *refs: kernel(count, *refs),
        out_shape=(
            jax.ShapeDtypeStruct((3, grains), F32),
            jax.ShapeDtypeStruct((1, contacts), F32),
        ),
        in_specs=[pl.BlockSpec(memory_space=pltpu.HBM)] * len(args),
        out_specs=(
            pl.BlockSpec(memory_space=pltpu.VMEM),
            pl.BlockSpec(memory_space=pltpu.VMEM),
        ),
        scratch_shapes=[pltpu.VMEM(arg.shape, arg.dtype) for arg in args]
        + [
            pltpu.VMEM((grains + 3 * width, contacts), BF16),
            pltpu.VMEM((4, grains, half), BF16),
            pltpu.VMEM((4, grains, half), BF16),
            pltpu.VMEM((2, grains, half), BF16),
            pltpu.VMEM((grains, width), BF16),
            pltpu.VMEM((4 * half, grains), BF16),
            pltpu.VMEM((4 * half, width), BF16),
            pltpu.VMEM((contacts, tile), BF16),
            pltpu.VMEM((contacts, tile), BF16),
            pltpu.VMEM((8, half), F32),
            pltpu.VMEM((8, grains), F32),
            pltpu.VMEM((8, width), F32),
            pltpu.VMEM((2, 8, width), F32),
            pltpu.VMEM((2, 8, width), F32),
            pltpu.VMEM((4, 8, half), F32),
            pltpu.VMEM((3, 3, half), jnp.int32),
            pltpu.VMEM((3, 8, grains), F32),
            pltpu.VMEM((2, 8, width), F32),
            pltpu.VMEM((4, 8, width), F32),
            pltpu.VMEM((2, 8, width), F32),
            pltpu.SemaphoreType.DMA((len(args),)),
            pltpu.SemaphoreType.DMA((MESSAGES,)),
            pltpu.SemaphoreType.DMA((MESSAGES,)),
        ],
        compiler_params=pltpu.CompilerParams(
            collective_id=0, has_side_effects=True, vmem_limit_bytes=32 << 20
        ),
        name="contact_step",
    )(*args)
    return current, lam.reshape(contacts)


def solution(mesh):
    count = mesh.shape["parts"]
    in_specs = (
        P(None, "parts"),
        P(None, "parts"),
        P("parts"),
        P(None, "parts"),
        P("parts"),
        P(None, "parts"),
        P("parts", None, None),
    )
    out_specs = (P(None, "parts"), P("parts"))
    return jax.shard_map(
        lambda *args: body(count, *args),
        mesh=mesh, in_specs=in_specs, out_specs=out_specs, check_vma=False,
    )
```

time: 44.3 us -> 39 us (0.88)
  the two profiles are of different devices: /device:TPU:1 before, /device:TPU:255 now
where the time goes in v2:
time: 39 us; the launch traced here: 38.9 us
  Pallas kernels  37.1 us (95%)
  local copies, waits for them, and re-layouts  1.19 us (3%)
  between operations  0.64 us (2%)
    pallas_call x1, Pallas kernels, body(): pl.pallas_call(lambda *refs: kernel(count, *refs), out_shape=(jax.ShapeDt...  37.1 us
    unnamed x2, local copies, waits for them, and re-layouts  1.19 us

profile of v2, /device:TPU:255, one launch (start us, length us, event | category | flops | bytes accessed | tf_op | source)
XLA Modules:
  0.0 38.9 jit_solution(11419641224167121025)
XLA Ops:
  0.6 37.1 %contact_step.1 = (f32[3,512]{1,0:T(4,128)S(1)}, f32[1,1024]{1,0:T(1,128)S(1)}) custom-call(f32[3,512]{1,0:T(4,128)} %refs_0_.1, f32[3,512]{1,0:T(4,128)} %refs_1_.1, f32[1,512]{1,0:T(1,128)} %bitcast.4, s32[3,256]{1,0:T(4,128)} %refs_3_.1, s32[1,128]{1,0:T(1,128)} %bitcast.5, s32[2,1024]{1,0:T(2,128)} %refs_5_.1, f32[8,128,128]{2,1,0:T(8,128)} %refs_6_.1), custom_call_target="tpu_custom_call" | custom-call | tf_op jit(solution)/shard_map/contact_step/pallas_call | solution.py:329
  37.7 0.6 %copy.11 = f32[3,512]{1,0:T(4,128)} copy(f32[3,512]{1,0:T(4,128)S(1)} %get-tuple-element.8) | data formatting | bytes 12288
  38.3 0.6 %copy.12 = f32[1024]{0:T(1024)} copy(f32[1024]{0:T(1024)S(1)} %bitcast.3) | data formatting | bytes 8192

commit v3 on v2

--- a/solution.py
+++ b/solution.py
@@ -62,7 +62,7 @@
     ends, tab0, tab1, tab2, rim_tab, slot_tab, edge_tab, tiles_hi, tiles_lo,
     send_a, send_k, send_r, send_c, send_f,
     recv_a, recv_l, recv_k, recv_r, recv_c, recv_f,
-    in_sem, send_sem, recv_sem,
+    in_sem, send_sem, recv_sem, far_sem,
 ):
     grains = pos_in.shape[1]
     half = lists_in.shape[1]
@@ -107,10 +107,11 @@
         for mask in masks:
             greet(flipped(me, far | mask))
 
-    for mask in masks[1:]:
+    for mask in (near, mid):
         greet(flipped(me, mask))
-    awaited = 3 + 4 * high.astype(jnp.int32)
-    for by in (1, -1, 2, -2):
+    pl.when(low)(lambda: greet(flipped(me, masks[3])))
+    awaited = 3 + 3 * high.astype(jnp.int32)
+    for by in (1, -1):
         pl.when(inside(by))(functools.partial(greet, shifted(me, by)))
         awaited += inside(by).astype(jnp.int32)
 
@@ -160,8 +161,17 @@
     send_a[...] = pick(state, tab0[0])
 
     pl.semaphore_wait(barrier, awaited)
-    pl.when(high)(lambda: send(0, 1, 2, 3))
-    send(4, 5, 6)
+
+    @pl.when(high)
+    def _():
+        for k in range(4):
+            pl.semaphore_signal(
+                far_sem.at[k], inc=1, device_id=(routes[k][2],), device_id_type=MESH
+            )
+        send(0, 1, 2, 3)
+
+    send(4, 5)
+    pl.when(low)(lambda: send(6))
     ones = jnp.ones((8, half), F32)
 
     def keep(table):
@@ -169,7 +179,13 @@
 
     kept = state * keep(tab0[0])
     send_k[...] = kept
-    send(7, 8, 9)
+    send(7, 8)
+    pl.when(low)(lambda: send(9))
+
+    @pl.when(high)
+    def _():
+        receive(4)
+        send(6, 9)
 
     pl.when(me < 1)(lambda: blank(recv_r.at[0], recv_c.at[0], recv_f.at[0]))
     pl.when(me > count - 2)(lambda: blank(recv_r.at[1], recv_c.at[1], recv_f.at[1]))
@@ -237,8 +253,10 @@
         return jnp.concatenate([rows, codes], axis=0)
 
     parts = [coded(0, kept)]
+    pl.when(low)(lambda: receive(4))
     for k in (1, 2, 3):
-        receive(3 + k)
+        if k > 1:
+            receive(3 + k)
         put_one_hot(tab0.at[k], recv_l[k - 1, 0:1, :])
         put_one_hot(tab1.at[k], recv_l[k - 1, 1:2, :])
         if k == 1:
@@ -261,11 +279,11 @@
 
     @pl.when(low)
     def _():
-        for k in (2, 3, 1, 0):
-            receive(k)
+        for k in range(4):
+            pl.semaphore_wait(far_sem.at[k], 1)
             send(k)
 
-    pl.when(high)(lambda: receive(2, 3, 1, 0))
+    receive(2, 3, 1, 0)
     arrived = split(jnp.concatenate([recv_a[k] for k in range(4)], axis=1))
     edge = edge[:8] + join(jnp.dot(arrived, edge_tab[...], preferred_element_type=F32))
     send_r[...] = edge
@@ -362,6 +380,7 @@
             pltpu.SemaphoreType.DMA((len(args),)),
             pltpu.SemaphoreType.DMA((MESSAGES,)),
             pltpu.SemaphoreType.DMA((MESSAGES,)),
+            pltpu.SemaphoreType.REGULAR((4,)),
         ],
         compiler_params=pltpu.CompilerParams(
             collective_id=0, has_side_effects=True, vmem_limit_bytes=32 << 20

time: 39 us -> 37.1 us (0.951)
  the two profiles are of different devices: /device:TPU:255 before, /device:TPU:384 now
where the time goes in v3:
time: 37.1 us; the launch traced here: 37 us
  Pallas kernels  35.1 us (95%)
  local copies, waits for them, and re-layouts  1.19 us (3%)
  between operations  0.64 us (2%)
    pallas_call x1, Pallas kernels, body(): pl.pallas_call(lambda *refs: kernel(count, *refs), out_shape=(jax.ShapeDt...  35.1 us
    unnamed x2, local copies, waits for them, and re-layouts  1.19 us

profile of v3, /device:TPU:384, one launch (start us, length us, event | category | flops | bytes accessed | tf_op | source)
XLA Modules:
  0.0 37.0 jit_solution(2390333118762580599)
XLA Ops:
  0.6 35.1 %contact_step.1 = (f32[3,512]{1,0:T(4,128)S(1)}, f32[1,1024]{1,0:T(1,128)S(1)}) custom-call(f32[3,512]{1,0:T(4,128)} %refs_0_.1, f32[3,512]{1,0:T(4,128)} %refs_1_.1, f32[1,512]{1,0:T(1,128)} %bitcast.4, s32[3,256]{1,0:T(4,128)} %refs_3_.1, s32[1,128]{1,0:T(1,128)} %bitcast.5, s32[2,1024]{1,0:T(2,128)} %refs_5_.1, f32[8,128,128]{2,1,0:T(8,128)} %refs_6_.1), custom_call_target="tpu_custom_call" | custom-call | tf_op jit(solution)/shard_map/contact_step/pallas_call | solution.py:347
  35.8 0.6 %copy.11 = f32[3,512]{1,0:T(4,128)} copy(f32[3,512]{1,0:T(4,128)S(1)} %get-tuple-element.8) | data formatting | bytes 12288
  36.4 0.6 %copy.12 = f32[1024]{0:T(1024)} copy(f32[1024]{0:T(1024)S(1)} %bitcast.3) | data formatting | bytes 8192

commit v4 on v3

--- a/solution.py
+++ b/solution.py
@@ -10,7 +10,7 @@
 MESH = pl.DeviceIdType.MESH
 F32 = jnp.float32
 BF16 = jnp.bfloat16
-MESSAGES = 18
+MESSAGES = 28
 
 
 def split(x):
@@ -59,10 +59,10 @@
     pos_hbm, vel_hbm, mass_hbm, lists_hbm, rim_hbm, pair_hbm, tiles_hbm,
     vel_out, lam_out,
     pos_in, vel_in, mass_in, lists_in, rim_in, pair_in, tiles_in,
-    ends, tab0, tab1, tab2, rim_tab, slot_tab, edge_tab, tiles_hi, tiles_lo,
-    send_a, send_k, send_r, send_c, send_f,
-    recv_a, recv_l, recv_k, recv_r, recv_c, recv_f,
-    in_sem, send_sem, recv_sem, far_sem,
+    ends, tab0, tab1, tab2, rim_tab, slot_tab, edge_tab, cross_tab, tiles_hi, tiles_lo,
+    send_a, send_k, send_r, send_c, send_f, send_e,
+    recv_a, recv_l, recv_k, recv_r, recv_c, recv_f, recv_x, recv_e, recv_p,
+    in_sem, send_sem, recv_sem, far_sem, edge_sem, hail_sem, near_sem, seen_sem,
 ):
     grains = pos_in.shape[1]
     half = lists_in.shape[1]
@@ -72,6 +72,7 @@
     bits = count.bit_length() - 1
     far, mid, near = (1 << (bits - 1 - level) for level in range(3))
     masks = (0, near, mid, mid | near)
+    plane = count // 16
     me = lax.axis_index("parts")
     high = me >= far
     low = me < far
@@ -82,8 +83,27 @@
     def flipped(base, mask):
         return lax.bitwise_xor(base, jnp.int32(mask))
 
+    def both(*conditions):
+        return functools.reduce(jnp.logical_and, conditions)
+
     def inside(by):
         return me >= -by if by < 0 else me < count - by
+
+    spot = lax.rem(me, plane)
+    top, bottom = spot == plane - 1, spot == 0
+    edge_side = jnp.where(top, 1, -1)
+    beyond = me + edge_side
+    across = jnp.logical_and(
+        jnp.logical_or(top, bottom), jnp.logical_and(beyond >= 0, beyond < count)
+    )
+    relays = [flipped(me, far | mask) + edge_side for mask in masks]
+    relayed = [
+        both(jnp.logical_or(both(top, high), bottom), to >= 0, to < count) for to in relays
+    ]
+    carrier = both(bottom, me > 0, me <= far)
+    carries = [flipped(me - carrier.astype(jnp.int32), far | mask) + 1 for mask in masks]
+    carried = [both(carrier, to < count) for to in carries]
+    served = both(bottom, me > far)
 
     loads = [
         pltpu.make_async_copy(src, dst, in_sem.at[i])
@@ -111,36 +131,69 @@
         greet(flipped(me, mask))
     pl.when(low)(lambda: greet(flipped(me, masks[3])))
     awaited = 3 + 3 * high.astype(jnp.int32)
-    for by in (1, -1):
-        pl.when(inside(by))(functools.partial(greet, shifted(me, by)))
-        awaited += inside(by).astype(jnp.int32)
-
-    routes = [(send_a, recv_a.at[k], flipped(me, far | masks[k]), 0) for k in range(4)]
-    routes += [(lists_in, recv_l.at[k - 1], flipped(me, masks[k]), 0) for k in (1, 2, 3)]
-    routes += [(send_k, recv_k.at[k - 1], flipped(me, masks[k]), 0) for k in (1, 2, 3)]
+    lower, upper = both(bottom, across), both(top, across)
+    for by, skipped, excused in ((1, upper, False), (-1, False, lower)):
+        pl.when(both(inside(by), jnp.logical_not(skipped)))(
+            functools.partial(greet, shifted(me, by))
+        )
+        awaited += both(inside(by), jnp.logical_not(excused)).astype(jnp.int32)
+    hailing = both(upper, beyond >= far)
+    awaited += 4 * hailing.astype(jnp.int32)
+    hailed = [jnp.logical_and(jnp.logical_and(low, bottom), condition) for condition in relayed]
+    for to, condition in zip(relays + carries, hailed + carried):
+        pl.when(condition)(functools.partial(greet, to))
+    awaited += 4 * served.astype(jnp.int32)
+
+    @pl.when(jnp.logical_and(across, beyond < far))
+    def _():
+        for mask in masks:
+            greet(flipped(beyond, far | mask))
+
+    for condition in relayed:
+        awaited += jnp.logical_and(high, condition).astype(jnp.int32)
+
+    routes = [(send_a, recv_a.at[k], flipped(me, far | masks[k]), None, None) for k in range(4)]
     routes += [
-        (send_r, recv_r.at[0], shifted(me, 1), 1),
-        (send_r, recv_r.at[1], shifted(me, -1), -1),
-        (send_c.at[0], recv_c.at[0], shifted(me, 1), 1),
-        (send_c.at[1], recv_c.at[1], shifted(me, -1), -1),
-        (send_c.at[0], recv_c.at[2], shifted(me, 2), 2),
-        (send_c.at[1], recv_c.at[3], shifted(me, -2), -2),
-        (send_f.at[0], recv_f.at[0], shifted(me, 1), 1),
-        (send_f.at[1], recv_f.at[1], shifted(me, -1), -1),
+        (src, dst.at[k - 1], flipped(me, masks[k]), None, None)
+        for src, dst in ((lists_in, recv_l), (send_k, recv_k))
+        for k in (1, 2, 3)
     ]
+    routes += [
+        (src, dst, shifted(me, by), inside(by), inside(-by))
+        for src, dst, by in (
+            (send_r, recv_r.at[0], 1),
+            (send_r, recv_r.at[1], -1),
+            (send_c.at[0], recv_c.at[0], 1),
+            (send_c.at[1], recv_c.at[1], -1),
+            (send_c.at[0], recv_c.at[2], 2),
+            (send_c.at[1], recv_c.at[3], -2),
+            (send_f.at[0], recv_f.at[0], 1),
+            (send_f.at[1], recv_f.at[1], -1),
+        )
+    ]
+    for i, out_gate, in_gate in ((10, top, bottom), (11, bottom, top)):
+        routes[i] = routes[i][:3] + tuple(
+            jnp.logical_and(condition, jnp.logical_not(gate))
+            for condition, gate in zip(routes[i][3:], (out_gate, in_gate))
+        )
+    direct = both(across, jnp.logical_not(served))
+    routes += [(send_a, recv_x.at[k], relays[k], relayed[k], direct) for k in range(4)]
+    routes += [(send_e, recv_e, beyond, across, across)]
+    routes += [(send_a, recv_p, beyond, both(top, low), carrier)]
+    routes += [(recv_p, recv_x.at[k], carries[k], carried[k], served) for k in range(4)]
     copies = [
         pltpu.make_async_remote_copy(
             src_ref=src, dst_ref=dst, send_sem=send_sem.at[i], recv_sem=recv_sem.at[i],
             device_id=(target,), device_id_type=MESH,
         )
-        for i, (src, dst, target, _) in enumerate(routes)
+        for i, (src, dst, target, _, _) in enumerate(routes)
     ]
 
-    def guarded(action, by):
-        if by == 0:
+    def guarded(action, condition):
+        if condition is None:
             action()
         else:
-            pl.when(inside(by))(action)
+            pl.when(condition)(action)
 
     def send(*which):
         for i in which:
@@ -148,7 +201,7 @@
 
     def receive(*which):
         for i in which:
-            guarded(copies[i].wait_recv, -routes[i][3])
+            guarded(copies[i].wait_recv, routes[i][4])
 
     def blank(*refs):
         for ref in refs:
@@ -162,13 +215,29 @@
 
     pl.semaphore_wait(barrier, awaited)
 
+    def tell(semaphore, peer):
+        pl.semaphore_signal(semaphore, inc=1, device_id=(peer,), device_id_type=MESH)
+
     @pl.when(high)
     def _():
         for k in range(4):
-            pl.semaphore_signal(
-                far_sem.at[k], inc=1, device_id=(routes[k][2],), device_id_type=MESH
-            )
-        send(0, 1, 2, 3)
+            tell(far_sem.at[k], routes[k][2])
+        tell(near_sem, flipped(me, near))
+        send(18, 19, 20, 21, 0, 1, 2, 3)
+
+    pl.when(upper)(lambda: tell(seen_sem, beyond))
+
+    send(23)
+
+    @pl.when(hailing)
+    def _():
+        for k in range(4):
+            tell(edge_sem.at[k], flipped(beyond, far | masks[k]))
+
+    @pl.when(served)
+    def _():
+        for k in range(4):
+            tell(hail_sem.at[k], flipped(me - 1, far | masks[k]) + 1)
 
     send(4, 5)
     pl.when(low)(lambda: send(6))
@@ -184,7 +253,7 @@
 
     @pl.when(high)
     def _():
-        receive(4)
+        pl.semaphore_wait(near_sem, 1)
         send(6, 9)
 
     pl.when(me < 1)(lambda: blank(recv_r.at[0], recv_c.at[0], recv_f.at[0]))
@@ -212,10 +281,10 @@
 
     extent = grains + 2 * width
     lax.fori_loop(0, extent // 32, put_ends, 0)
-    across = lax.broadcasted_iota(jnp.int32, (width, width), 0) == lax.broadcasted_iota(
+    square = lax.broadcasted_iota(jnp.int32, (width, width), 0) == lax.broadcasted_iota(
         jnp.int32, (width, width), 1
     )
-    rim_column = jnp.sum(jnp.where(across, rim_row, 0), axis=1, keepdims=True)
+    rim_column = jnp.sum(jnp.where(square, rim_row, 0), axis=1, keepdims=True)
     for i in range(0, width, 32):
         ends[extent + i : extent + i + 32, :] = touch(rim_column[i : i + 32])
 
@@ -252,11 +321,25 @@
         codes = spread(jnp.where(code_row == k, order, 0.0), tab0[k])
         return jnp.concatenate([rows, codes], axis=0)
 
+    def answer():
+        for k in range(4):
+            pl.semaphore_wait(far_sem.at[k], 1)
+            send(k)
+
+    def carry():
+        receive(23)
+        for k in range(4):
+
+            @pl.when(carried[k])
+            def _():
+                pl.semaphore_wait(hail_sem.at[k], 1)
+                copies[24 + k].start()
+
+    pl.when(both(low, me >= far // 2))(answer)
+    pl.when(both(carrier, me >= far // 2))(carry)
     parts = [coded(0, kept)]
-    pl.when(low)(lambda: receive(4))
     for k in (1, 2, 3):
-        if k > 1:
-            receive(3 + k)
+        receive(3 + k)
         put_one_hot(tab0.at[k], recv_l[k - 1, 0:1, :])
         put_one_hot(tab1.at[k], recv_l[k - 1, 1:2, :])
         if k == 1:
@@ -269,6 +352,9 @@
     ]
     state = pair[0] * keep(tab2[0]) + spread(pick(pair[1], tab2[1]), tab2[0])
     edge = pick(state, rim_tab[...])
+    send_e[...] = edge
+    pl.when(lower)(lambda: pl.semaphore_wait(seen_sem, 1))
+    send(22)
     for k in range(4):
         put_one_hot(
             edge_tab.at[k * half : (k + 1) * half, :], edge[8 + k : 9 + k].astype(jnp.int32), 1
@@ -277,11 +363,14 @@
             slot_tab.at[k * half : (k + 1) * half, :], state[8 + k : 9 + k].astype(jnp.int32), 1
         )
 
-    @pl.when(low)
-    def _():
-        for k in range(4):
-            pl.semaphore_wait(far_sem.at[k], 1)
-            send(k)
+    pl.when(me < far // 2)(answer)
+    pl.when(both(carrier, me < far // 2))(carry)
+    for k in range(4):
+
+        @pl.when(hailed[k])
+        def _():
+            pl.semaphore_wait(edge_sem.at[k], 1)
+            copies[18 + k].start()
 
     receive(2, 3, 1, 0)
     arrived = split(jnp.concatenate([recv_a[k] for k in range(4)], axis=1))
@@ -291,6 +380,20 @@
     state = state[:8] + join(jnp.dot(arrived, slot_tab[...], preferred_element_type=F32))
     vel, mass = state[3:6], state[6:7]
     gathered = pick(state, ends[:grains, :])
+
+    @pl.when(across)
+    def _():
+        receive(22)
+        for k in range(4):
+            put_one_hot(
+                cross_tab.at[k * half : (k + 1) * half, :],
+                recv_e[8 + k : 9 + k, :].astype(jnp.int32), 1,
+            )
+        receive(20, 21, 19, 18, 26, 27, 25, 24)
+        seen = split(jnp.concatenate([recv_x[k] for k in range(4)], axis=1))
+        recv_r[top.astype(jnp.int32)] = recv_e[:8] + join(
+            jnp.dot(seen, cross_tab[...], preferred_element_type=F32)
+        )
 
     receive(10, 11)
     left, right = recv_r[0], recv_r[1]
@@ -364,6 +467,7 @@
             pltpu.VMEM((grains, width), BF16),
             pltpu.VMEM((4 * half, grains), BF16),
             pltpu.VMEM((4 * half, width), BF16),
+            pltpu.VMEM((4 * half, width), BF16),
             pltpu.VMEM((contacts, tile), BF16),
             pltpu.VMEM((contacts, tile), BF16),
             pltpu.VMEM((8, half), F32),
@@ -371,16 +475,24 @@
             pltpu.VMEM((8, width), F32),
             pltpu.VMEM((2, 8, width), F32),
             pltpu.VMEM((2, 8, width), F32),
+            pltpu.VMEM((16, width), F32),
             pltpu.VMEM((4, 8, half), F32),
             pltpu.VMEM((3, 3, half), jnp.int32),
             pltpu.VMEM((3, 8, grains), F32),
             pltpu.VMEM((2, 8, width), F32),
             pltpu.VMEM((4, 8, width), F32),
             pltpu.VMEM((2, 8, width), F32),
+            pltpu.VMEM((4, 8, half), F32),
+            pltpu.VMEM((16, width), F32),
+            pltpu.VMEM((8, half), F32),
             pltpu.SemaphoreType.DMA((len(args),)),
             pltpu.SemaphoreType.DMA((MESSAGES,)),
             pltpu.SemaphoreType.DMA((MESSAGES,)),
             pltpu.SemaphoreType.REGULAR((4,)),
+            pltpu.SemaphoreType.REGULAR((4,)),
+            pltpu.SemaphoreType.REGULAR((4,)),
+            pltpu.SemaphoreType.REGULAR,
+            pltpu.SemaphoreType.REGULAR,
         ],
         compiler_params=pltpu.CompilerParams(
             collective_id=0, has_side_effects=True, vmem_limit_bytes=32 << 20

time: 37.1 us -> 36.8 us (level)
  the two profiles are of different devices: /device:TPU:384 before, /device:TPU:127 now
where the time goes in v4:
time: 36.8 us; the launch traced here: 36.6 us
  Pallas kernels  34.8 us (95%)
  local copies, waits for them, and re-layouts  1.19 us (3%)
  between operations  0.64 us (2%)
    pallas_call x1, Pallas kernels, body(): pl.pallas_call(lambda *refs: kernel(count, *refs), out_shape=(jax.ShapeDt...  34.8 us
    unnamed x2, local copies, waits for them, and re-layouts  1.19 us

profile of v4, /device:TPU:127, one launch (start us, length us, event | category | flops | bytes accessed | tf_op | source)
XLA Modules:
  0.0 36.6 jit_solution(18404130339237179380)
XLA Ops:
  0.6 34.8 %contact_step.1 = (f32[3,512]{1,0:T(4,128)S(1)}, f32[1,1024]{1,0:T(1,128)S(1)}) custom-call(f32[3,512]{1,0:T(4,128)} %refs_0_.1, f32[3,512]{1,0:T(4,128)} %refs_1_.1, f32[1,512]{1,0:T(1,128)} %bitcast.4, s32[3,256]{1,0:T(4,128)} %refs_3_.1, s32[1,128]{1,0:T(1,128)} %bitcast.5, s32[2,1024]{1,0:T(2,128)} %refs_5_.1, f32[8,128,128]{2,1,0:T(8,128)} %refs_6_.1), custom_call_target="tpu_custom_call" | custom-call | tf_op jit(solution)/shard_map/contact_step/pallas_call | solution.py:450
  35.4 0.6 %copy.11 = f32[3,512]{1,0:T(4,128)} copy(f32[3,512]{1,0:T(4,128)S(1)} %get-tuple-element.8) | data formatting | bytes 12288
  36.0 0.6 %copy.12 = f32[1024]{0:T(1024)} copy(f32[1024]{0:T(1024)S(1)} %bitcast.3) | data formatting | bytes 8192

commit v5 on v4

--- a/solution.py
+++ b/solution.py
@@ -97,8 +97,22 @@
         jnp.logical_or(top, bottom), jnp.logical_and(beyond >= 0, beyond < count)
     )
     relays = [flipped(me, far | mask) + edge_side for mask in masks]
+    early = far // 2
+
+    def quick(part):
+        return functools.reduce(
+            jnp.logical_or, [part <= early, part == far - 1, part > far]
+        )
+
+    mine, theirs = both(across, quick(me)), both(across, quick(beyond))
     relayed = [
-        both(jnp.logical_or(both(top, high), bottom), to >= 0, to < count) for to in relays
+        both(
+            to >= 0,
+            jnp.logical_or(
+                both(high, jnp.logical_or(top, bottom), to <= early), both(low, bottom)
+            ),
+        )
+        for to in relays
     ]
     carrier = both(bottom, me > 0, me <= far)
     carries = [flipped(me - carrier.astype(jnp.int32), far | mask) + 1 for mask in masks]
@@ -144,7 +158,7 @@
         pl.when(condition)(functools.partial(greet, to))
     awaited += 4 * served.astype(jnp.int32)
 
-    @pl.when(jnp.logical_and(across, beyond < far))
+    @pl.when(both(across, me <= early))
     def _():
         for mask in masks:
             greet(flipped(beyond, far | mask))
@@ -173,12 +187,14 @@
     ]
     for i, out_gate, in_gate in ((10, top, bottom), (11, bottom, top)):
         routes[i] = routes[i][:3] + tuple(
-            jnp.logical_and(condition, jnp.logical_not(gate))
-            for condition, gate in zip(routes[i][3:], (out_gate, in_gate))
-        )
-    direct = both(across, jnp.logical_not(served))
+            both(condition, jnp.logical_not(both(gate, hurried)))
+            for condition, gate, hurried in zip(
+                routes[i][3:], (out_gate, in_gate), (theirs, mine)
+            )
+        )
+    direct = both(mine, jnp.logical_not(served))
     routes += [(send_a, recv_x.at[k], relays[k], relayed[k], direct) for k in range(4)]
-    routes += [(send_e, recv_e, beyond, across, across)]
+    routes += [(send_e, recv_e, beyond, theirs, mine)]
     routes += [(send_a, recv_p, beyond, both(top, low), carrier)]
     routes += [(recv_p, recv_x.at[k], carries[k], carried[k], served) for k in range(4)]
     copies = [
@@ -335,8 +351,8 @@
                 pl.semaphore_wait(hail_sem.at[k], 1)
                 copies[24 + k].start()
 
-    pl.when(both(low, me >= far // 2))(answer)
-    pl.when(both(carrier, me >= far // 2))(carry)
+    pl.when(both(low, me >= early))(answer)
+    pl.when(both(carrier, me >= early))(carry)
     parts = [coded(0, kept)]
     for k in (1, 2, 3):
         receive(3 + k)
@@ -363,8 +379,8 @@
             slot_tab.at[k * half : (k + 1) * half, :], state[8 + k : 9 + k].astype(jnp.int32), 1
         )
 
-    pl.when(me < far // 2)(answer)
-    pl.when(both(carrier, me < far // 2))(carry)
+    pl.when(me < early)(answer)
+    pl.when(both(carrier, me < early))(carry)
     for k in range(4):
 
         @pl.when(hailed[k])
@@ -381,7 +397,7 @@
     vel, mass = state[3:6], state[6:7]
     gathered = pick(state, ends[:grains, :])
 
-    @pl.when(across)
+    @pl.when(mine)
     def _():
         receive(22)
         for k in range(4):

time: 36.8 us -> 35.1 us (0.954)
  the two profiles are of different devices: /device:TPU:127 before, /device:TPU:160 now
where the time goes in v5:
time: 35.1 us; the launch traced here: 34.9 us
  Pallas kernels  33.1 us (94%)
  local copies, waits for them, and re-layouts  1.19 us (3%)
  between operations  0.64 us (2%)
    pallas_call x1, Pallas kernels, body(): pl.pallas_call(lambda *refs: kernel(count, *refs), out_shape=(jax.ShapeDt...  33.1 us
    unnamed x2, local copies, waits for them, and re-layouts  1.19 us

profile of v5, /device:TPU:160, one launch (start us, length us, event | category | flops | bytes accessed | tf_op | source)
XLA Modules:
  0.0 34.9 jit_solution(706453740046356901)
XLA Ops:
  0.6 33.1 %contact_step.1 = (f32[3,512]{1,0:T(4,128)S(1)}, f32[1,1024]{1,0:T(1,128)S(1)}) custom-call(f32[3,512]{1,0:T(4,128)} %refs_0_.1, f32[3,512]{1,0:T(4,128)} %refs_1_.1, f32[1,512]{1,0:T(1,128)} %bitcast.4, s32[3,256]{1,0:T(4,128)} %refs_3_.1, s32[1,128]{1,0:T(1,128)} %bitcast.5, s32[2,1024]{1,0:T(2,128)} %refs_5_.1, f32[8,128,128]{2,1,0:T(8,128)} %refs_6_.1), custom_call_target="tpu_custom_call" | custom-call | tf_op jit(solution)/shard_map/contact_step/pallas_call | solution.py:466
  33.7 0.6 %copy.11 = f32[3,512]{1,0:T(4,128)} copy(f32[3,512]{1,0:T(4,128)S(1)} %get-tuple-element.8) | data formatting | bytes 12288
  34.3 0.6 %copy.12 = f32[1024]{0:T(1024)} copy(f32[1024]{0:T(1024)S(1)} %bitcast.3) | data formatting | bytes 8192

commit v6 on v5

--- a/solution.py
+++ b/solution.py
@@ -101,7 +101,7 @@
 
     def quick(part):
         return functools.reduce(
-            jnp.logical_or, [part <= early, part == far - 1, part > far]
+            jnp.logical_or, [part <= early, part == far - 1, part > far, part == early + plane]
         )
 
     mine, theirs = both(across, quick(me)), both(across, quick(beyond))
@@ -109,7 +109,8 @@
         both(
             to >= 0,
             jnp.logical_or(
-                both(high, jnp.logical_or(top, bottom), to <= early), both(low, bottom)
+                both(high, jnp.logical_or(top, bottom), to < far - 1, quick(to)),
+                both(low, bottom),
             ),
         )
         for to in relays
@@ -158,7 +159,7 @@
         pl.when(condition)(functools.partial(greet, to))
     awaited += 4 * served.astype(jnp.int32)
 
-    @pl.when(both(across, me <= early))
+    @pl.when(both(mine, me < far - 1))
     def _():
         for mask in masks:
             greet(flipped(beyond, far | mask))
@@ -236,10 +237,11 @@
 
     @pl.when(high)
     def _():
+        send(18, 19, 20, 21)
         for k in range(4):
             tell(far_sem.at[k], routes[k][2])
+        send(0, 1, 2, 3)
         tell(near_sem, flipped(me, near))
-        send(18, 19, 20, 21, 0, 1, 2, 3)
 
     pl.when(upper)(lambda: tell(seen_sem, beyond))
 

time: 35.1 us -> 34.8 us (level)
  the two profiles are of different devices: /device:TPU:160 before, /device:TPU:32 now
where the time goes in v6:
time: 34.8 us; the launch traced here: 34.7 us
  Pallas kernels  32.9 us (95%)
  local copies, waits for them, and re-layouts  1.19 us (3%)
  between operations  0.64 us (2%)
    pallas_call x1, Pallas kernels, body(): pl.pallas_call(lambda *refs: kernel(count, *refs), out_shape=(jax.ShapeDt...  32.9 us
    unnamed x2, local copies, waits for them, and re-layouts  1.19 us

profile of v6, /device:TPU:32, one launch (start us, length us, event | category | flops | bytes accessed | tf_op | source)
XLA Modules:
  0.0 34.7 jit_solution(7122977934038469430)
XLA Ops:
  0.6 32.9 %contact_step.1 = (f32[3,512]{1,0:T(4,128)S(1)}, f32[1,1024]{1,0:T(1,128)S(1)}) custom-call(f32[3,512]{1,0:T(4,128)} %refs_0_.1, f32[3,512]{1,0:T(4,128)} %refs_1_.1, f32[1,512]{1,0:T(1,128)} %bitcast.4, s32[3,256]{1,0:T(4,128)} %refs_3_.1, s32[1,128]{1,0:T(1,128)} %bitcast.5, s32[2,1024]{1,0:T(2,128)} %refs_5_.1, f32[8,128,128]{2,1,0:T(8,128)} %refs_6_.1), custom_call_target="tpu_custom_call" | custom-call | tf_op jit(solution)/shard_map/contact_step/pallas_call | solution.py:468
  33.5 0.6 %copy.11 = f32[3,512]{1,0:T(4,128)} copy(f32[3,512]{1,0:T(4,128)S(1)} %get-tuple-element.8) | data formatting | bytes 12288
  34.1 0.6 %copy.12 = f32[1024]{0:T(1024)} copy(f32[1024]{0:T(1024)S(1)} %bitcast.3) | data formatting | bytes 8192

commit v7 on v6

--- a/solution.py
+++ b/solution.py
@@ -451,6 +451,17 @@
     vel_out[...] = base + mass * spread(recv_f[0] + recv_f[1], rim_tab[...])[0:3]
     for i in range(MESSAGES):
         guarded(copies[i].wait_send, routes[i][3])
+
+
+def settle(vel_ref, lam_ref, vel_out, lam_out, sem):
+    moves = [
+        pltpu.make_async_copy(vel_ref, vel_out, sem.at[0]),
+        pltpu.make_async_copy(lam_ref, lam_out, sem.at[1]),
+    ]
+    for move in moves:
+        move.start()
+    for move in moves:
+        move.wait()
 
 
 def body(count, positions, velocity, inv_mass, swap_lists, rim_list, contact_pair, delassus):
@@ -517,6 +528,22 @@
         ),
         name="contact_step",
     )(*args)
+    current, lam = pl.pallas_call(
+        settle,
+        out_shape=(
+            jax.ShapeDtypeStruct((3, grains), F32),
+            jax.ShapeDtypeStruct((1, contacts), F32),
+        ),
+        in_specs=[pl.BlockSpec(memory_space=pl.ANY)] * 2,
+        out_specs=(
+            pl.BlockSpec(memory_space=pltpu.HBM), pl.BlockSpec(memory_space=pltpu.HBM)
+        ),
+        scratch_shapes=[pltpu.SemaphoreType.DMA((2,))],
+        name="settle",
+    )(
+        pltpu.with_memory_space_constraint(current, pltpu.VMEM),
+        pltpu.with_memory_space_constraint(lam, pltpu.VMEM),
+    )
     return current, lam.reshape(contacts)
 
 

time: 34.8 us -> 34.3 us (0.986)
  local copies, waits for them, and re-layouts: 1.19 us -> 0 us
  Pallas kernels: 32.9 us -> 33.5 us
    unnamed x2 -> x0, local copies, waits for them, and re-layouts: 1.19 us -> none
    pallas_call x0 -> x1, Pallas kernels: none -> 0.62 us  [body(): pl.pallas_call(settle, out_shape=(jax.ShapeDtypeStruct((3, grains), F32),...]
where the time goes in v7:
time: 34.3 us; the launch traced here: 34.1 us
  Pallas kernels  33.5 us (98%)
  between operations  0.64 us (2%)
    pallas_call x1, Pallas kernels, body(): pl.pallas_call(lambda *refs: kernel(count, *refs), out_shape=(jax.ShapeDt...  32.9 us

profile of v7, /device:TPU:32, one launch (start us, length us, event | category | flops | bytes accessed | tf_op | source)
XLA Modules:
  0.0 34.1 jit_solution(2842580212730643594)
XLA Ops:
  0.6 32.9 %contact_step.1 = (f32[3,512]{1,0:T(4,128)S(1)}, f32[1,1024]{1,0:T(1,128)S(1)}) custom-call(f32[3,512]{1,0:T(4,128)} %refs_0_.1, f32[3,512]{1,0:T(4,128)} %refs_1_.1, f32[1,512]{1,0:T(1,128)} %bitcast.3, s32[3,256]{1,0:T(4,128)} %refs_3_.1, s32[1,128]{1,0:T(1,128)} %bitcast.4, s32[2,1024]{1,0:T(2,128)} %refs_5_.1, f32[8,128,128]{2,1,0:T(8,128)} %refs_6_.1), custom_call_target="tpu_custom_call" | custom-call | tf_op jit(solution)/shard_map/contact_step/pallas_call | solution.py:479
  33.5 0.6 %settle.1 = (f32[3,512]{1,0:T(4,128)}, f32[1,1024]{1,0:T(1,128)}) custom-call(f32[3,512]{1,0:T(4,128)S(1)} %get-tuple-element.6.vel_ref, f32[1,1024]{1,0:T(1,128)S(1)} %get-tuple-element.7.lam_ref), custom_call_target="tpu_custom_call" | custom-call | tf_op jit(solution)/shard_map/settle/pallas_call | solution.py:531

commit v8 on v7

--- a/solution.py
+++ b/solution.py
@@ -129,7 +129,7 @@
             ]
         )
     ]
-    for load in loads:
+    for load in loads[:4]:
         load.start()
 
     barrier = pltpu.get_barrier_semaphore()
@@ -220,6 +220,10 @@
         for i in which:
             guarded(copies[i].wait_recv, routes[i][4])
 
+    def settled(*which):
+        for i in which:
+            guarded(copies[i].wait_send, routes[i][3])
+
     def blank(*refs):
         for ref in refs:
             ref[...] = jnp.zeros(ref.shape, F32)
@@ -257,6 +261,8 @@
         for k in range(4):
             tell(hail_sem.at[k], flipped(me - 1, far | masks[k]) + 1)
 
+    for load in loads[4:]:
+        load.start()
     send(4, 5)
     pl.when(low)(lambda: send(6))
     ones = jnp.ones((8, half), F32)
@@ -446,11 +452,11 @@
     send(16, 17)
     lam_out[...] = lam
     base = vel + mass * spread(force, ends[:grains, :])[0:3]
+    settled(*range(16), *range(18, MESSAGES))
 
     receive(16, 17)
     vel_out[...] = base + mass * spread(recv_f[0] + recv_f[1], rim_tab[...])[0:3]
-    for i in range(MESSAGES):
-        guarded(copies[i].wait_send, routes[i][3])
+    settled(16, 17)
 
 
 def settle(vel_ref, lam_ref, vel_out, lam_out, sem):

time: 34.3 us -> 34.2 us (level)
  no operation moved by 1% of the time
where the time goes in v8:
time: 34.2 us; the launch traced here: 34.1 us
  Pallas kernels  33.4 us (98%)
  between operations  0.64 us (2%)
    pallas_call x1, Pallas kernels, body(): pl.pallas_call(lambda *refs: kernel(count, *refs), out_shape=(jax.ShapeDt...  32.8 us

profile of v8, /device:TPU:32, one launch (start us, length us, event | category | flops | bytes accessed | tf_op | source)
XLA Modules:
  0.0 34.1 jit_solution(2129701965001171579)
XLA Ops:
  0.6 32.8 %contact_step.1 = (f32[3,512]{1,0:T(4,128)S(1)}, f32[1,1024]{1,0:T(1,128)S(1)}) custom-call(f32[3,512]{1,0:T(4,128)} %refs_0_.1, f32[3,512]{1,0:T(4,128)} %refs_1_.1, f32[1,512]{1,0:T(1,128)} %bitcast.3, s32[3,256]{1,0:T(4,128)} %refs_3_.1, s32[1,128]{1,0:T(1,128)} %bitcast.4, s32[2,1024]{1,0:T(2,128)} %refs_5_.1, f32[8,128,128]{2,1,0:T(8,128)} %refs_6_.1), custom_call_target="tpu_custom_call" | custom-call | tf_op jit(solution)/shard_map/contact_step/pallas_call | solution.py:485
  33.4 0.6 %settle.1 = (f32[3,512]{1,0:T(4,128)}, f32[1,1024]{1,0:T(1,128)}) custom-call(f32[3,512]{1,0:T(4,128)S(1)} %get-tuple-element.6.vel_ref, f32[1,1024]{1,0:T(1,128)S(1)} %get-tuple-element.7.lam_ref), custom_call_target="tpu_custom_call" | custom-call | tf_op jit(solution)/shard_map/settle/pallas_call | solution.py:537

commit v9 on v8

--- a/solution.py
+++ b/solution.py
@@ -129,7 +129,7 @@
             ]
         )
     ]
-    for load in loads[:4]:
+    for load in loads:
         load.start()
 
     barrier = pltpu.get_barrier_semaphore()
@@ -261,8 +261,6 @@
         for k in range(4):
             tell(hail_sem.at[k], flipped(me - 1, far | masks[k]) + 1)
 
-    for load in loads[4:]:
-        load.start()
     send(4, 5)
     pl.when(low)(lambda: send(6))
     ones = jnp.ones((8, half), F32)

time: 34.2 us -> 34.2 us (level)
  no operation moved by 1% of the time
where the time goes in v9:
time: 34.2 us; the launch traced here: 34.1 us
  Pallas kernels  33.4 us (98%)
  between operations  0.64 us (2%)
    pallas_call x1, Pallas kernels, body(): pl.pallas_call(lambda *refs: kernel(count, *refs), out_shape=(jax.ShapeDt...  32.8 us

profile of v9, /device:TPU:32, one launch (start us, length us, event | category | flops | bytes accessed | tf_op | source)
XLA Modules:
  0.0 34.1 jit_solution(9851958649200987807)
XLA Ops:
  0.6 32.8 %contact_step.1 = (f32[3,512]{1,0:T(4,128)S(1)}, f32[1,1024]{1,0:T(1,128)S(1)}) custom-call(f32[3,512]{1,0:T(4,128)} %refs_0_.1, f32[3,512]{1,0:T(4,128)} %refs_1_.1, f32[1,512]{1,0:T(1,128)} %bitcast.3, s32[3,256]{1,0:T(4,128)} %refs_3_.1, s32[1,128]{1,0:T(1,128)} %bitcast.4, s32[2,1024]{1,0:T(2,128)} %refs_5_.1, f32[8,128,128]{2,1,0:T(8,128)} %refs_6_.1), custom_call_target="tpu_custom_call" | custom-call | tf_op jit(solution)/shard_map/contact_step/pallas_call | solution.py:483
  33.4 0.6 %settle.1 = (f32[3,512]{1,0:T(4,128)}, f32[1,1024]{1,0:T(1,128)}) custom-call(f32[3,512]{1,0:T(4,128)S(1)} %get-tuple-element.6.vel_ref, f32[1,1024]{1,0:T(1,128)S(1)} %get-tuple-element.7.lam_ref), custom_call_target="tpu_custom_call" | custom-call | tf_op jit(solution)/shard_map/settle/pallas_call | solution.py:535
